TPU v7x, 256 devices: a whole 4x4x8 slice. The times are simulated.
256 devices in a mesh: gz: 32 (over x_hi, z, core), gy: 8 (over x_lo, y).
Axes of the slice: x: 4 (x_hi: 2, x_lo: 2; x = x_hi * 2 + x_lo), y: 4, z: 8, core: 2. Of those that a mesh axis runs over, the one named last changes fastest.
Arguments:
- level_set: float32 [512, 256, 256], P('gz', 'gy'), may hold values from -8 to 8
Outputs:
- reinitialized: float32 [512, 256, 256], P('gz', 'gy')
All inputs are finite; a program needn't handle non-finite values.
Results may differ from a plain program's by a relative error of at most 0.0003.
Values sent between devices are 32-bit elements; how exact they have to be, the bound alone decides.
No kernel may reach another device: no remote copies, remote signals or barrier semaphores. Data moves between devices by JAX's collectives and lax.ppermute only.
A program may use at most 64 MiB of HBM per device.

v0:
```python
import jax
import jax.numpy as jnp
from jax import lax
from jax.sharding import PartitionSpec as P

STEPS = 2


weno_eps = 1e-06
pseudo_step = 0.3


def padded_2(block, sides, width, periodic):
    for axis, dim in sides:
        count = lax.axis_size(axis)
        forward = [(i, i + 1) for i in range(count - 1)]
        if periodic:
            forward.append((count - 1, 0))
        backward = [(target, source) for source, target in forward]
        low = lax.ppermute(
            lax.slice_in_dim(block, block.shape[dim] - width, None, axis=dim), axis, forward
        )
        high = lax.ppermute(lax.slice_in_dim(block, 0, width, axis=dim), axis, backward)
        block = jnp.concatenate([low, block, high], axis=dim)
    return block


def weno_five(first, second, third, fourth, fifth):
    cand_one = first / 3.0 - 7.0 * second / 6.0 + 11.0 * third / 6.0
    cand_two = -second / 6.0 + 5.0 * third / 6.0 + fourth / 3.0
    cand_three = third / 3.0 + 5.0 * fourth / 6.0 - fifth / 6.0
    smooth_one = (
        13.0 / 12.0 * (first - 2.0 * second + third) ** 2
        + 0.25 * (first - 4.0 * second + 3.0 * third) ** 2
    )
    smooth_two = 13.0 / 12.0 * (second - 2.0 * third + fourth) ** 2 + 0.25 * (second - fourth) ** 2
    smooth_three = (
        13.0 / 12.0 * (third - 2.0 * fourth + fifth) ** 2
        + 0.25 * (3.0 * third - 4.0 * fourth + fifth) ** 2
    )
    alpha_one = 0.1 / (weno_eps + smooth_one) ** 2
    alpha_two = 0.6 / (weno_eps + smooth_two) ** 2
    alpha_three = 0.3 / (weno_eps + smooth_three) ** 2
    total = alpha_one + alpha_two + alpha_three
    return (alpha_one * cand_one + alpha_two * cand_two + alpha_three * cand_three) / total


def weno_pair(padded, axis):
    length = padded.shape[axis] - 6
    diffs = jnp.diff(padded, axis=axis)
    parts = [lax.slice_in_dim(diffs, k, k + length, axis=axis) for k in range(6)]
    backward = weno_five(parts[0], parts[1], parts[2], parts[3], parts[4])
    forward = weno_five(parts[5], parts[4], parts[3], parts[2], parts[1])
    return (backward, forward)


def godunov(backward, forward, positive):
    plus_case = jnp.maximum(jnp.maximum(backward, 0.0) ** 2, jnp.minimum(forward, 0.0) ** 2)
    minus_case = jnp.maximum(jnp.minimum(backward, 0.0) ** 2, jnp.maximum(forward, 0.0) ** 2)
    return jnp.where(positive, plus_case, minus_case)


def rate(z_ext, y_ext, center, sign):
    positive = sign >= 0.0
    back_z, fore_z = weno_pair(z_ext, 0)
    back_y, fore_y = weno_pair(y_ext, 1)
    x_ext = jnp.pad(center, ((0, 0), (0, 0), (3, 3)), mode="edge")
    back_x, fore_x = weno_pair(x_ext, 2)
    squared = (
        godunov(back_z, fore_z, positive)
        + godunov(back_y, fore_y, positive)
        + godunov(back_x, fore_x, positive)
    )
    return -sign * (jnp.sqrt(squared) - 1.0)


def fix_edges(field, margin):
    inner_rows = field.shape[1] - 2 * margin
    position = lax.axis_index("gy")
    is_first = position == 0
    is_last = position == lax.axis_size("gy") - 1
    rows = lax.broadcasted_iota(jnp.int32, field.shape, 1)
    low_plane = field[:, margin : margin + 1]
    high_plane = field[:, margin + inner_rows - 1 : margin + inner_rows]
    field = jnp.where(is_first & (rows < margin), low_plane, field)
    field = jnp.where(is_last & (rows >= margin + inner_rows), high_plane, field)
    return field


def section_rate(field, sign):
    z_ext = padded_2(field, (("gz", 0),), 3, True)
    y_ext = padded_2(field, (("gy", 1),), 3, False)
    y_ext = fix_edges(y_ext, 3)
    return rate(z_ext, y_ext, field, sign)


def per_device(level_set):
    field = level_set
    sign = level_set / jnp.sqrt(level_set * level_set + 1.0)
    for step in range(STEPS):
        first = field + pseudo_step * section_rate(field, sign)
        second = 0.75 * field + 0.25 * (first + pseudo_step * section_rate(first, sign))
        field = 1.0 / 3.0 * field + 2.0 / 3.0 * (second + pseudo_step * section_rate(second, sign))
    return field


def solution(mesh):
    return jax.shard_map(
        per_device,
        mesh=mesh,
        in_specs=(P("gz", "gy", None),),
        out_specs=P("gz", "gy", None),
        check_vma=False,
    )
```

profile of v0, /device:TPU:2, one launch (start us, length us, event | category | flops | bytes accessed | tf_op | source)
XLA Modules:
  0.0 150.6 jit_solution(10478674457460185336)
XLA Ops:
  1.4 3.6 %collective-permute-start.2 = (f32[16,3,256]{2,0,1:T(8,128)S(1)}, f32[16,3,256]{2,0,1:T(8,128)S(1)}, u32[]{:S(2)}, u32[]{:S(2)}) collective-permute-start(f32[16,3,256]{2,0,1:T(8,128)S(1)} %get-tuple-element.49), channel_id=1, source_target_pairs={{0,1},{1,2},{2,3},{3,4},{4,5},{5,6},{6,7},{8,9},{9,10},{10,11},{11... | collective-permute-start | bytes 147464 | tf_op jit(solution)/shard_map/ppermute | solution.py:20
  5.0 4.5 %collective-permute-start.3 = (f32[16,3,256]{2,0,1:T(8,128)S(1)}, f32[16,3,256]{2,0,1:T(8,128)S(1)}, u32[]{:S(2)}, u32[]{:S(2)}) collective-permute-start(f32[16,3,256]{2,0,1:T(8,128)S(1)} %get-tuple-element.50), channel_id=1, source_target_pairs={{1,0},{2,1},{3,2},{4,3},{5,4},{6,5},{7,6},{9,8},{10,9},{11,10},{12... | collective-permute-start | bytes 147464 | tf_op jit(solution)/shard_map/ppermute | solution.py:23
  9.6 6.4 %collective-permute-start.1 = (f32[3,32,256]{2,0,1:T(4,128)S(1)}, f32[3,32,256]{2,0,1:T(4,128)S(1)}, u32[]{:S(2)}, u32[]{:S(2)}) collective-permute-start(f32[3,32,256]{2,0,1:T(4,128)S(1)} %get-tuple-element.46), channel_id=1, source_target_pairs={{8,0},{16,8},{24,16},{32,24},{40,32},{48,40},{56,48},{64,56},{72,6... | collective-permute-start | bytes 294920 | tf_op jit(solution)/shard_map/ppermute | solution.py:23
  18.8 8.0 %multiply_add_fusion.5 = f32[16,32,256]{2,0,1:T(8,128)S(1)} fusion(f32[16,32,261]{2,0,1:T(8,128)S(1)} %slice_subtract_fusion.10, f32[16,37,256]{2,0,1:T(8,128)S(1)} %slice_subtract_fusion.17, f32[21,32,256]{2,0,1:T(8,128)S(1)} %slice_subtract_fusion.11, f32[16,32,256]{2,1,0:T(8,128)S(1)} %copy-done), kind=kLoop, calls=%fused_computation.47 | loop fusion | flops 54525952 | bytes 10485760 | tf_op jit(solution)/shard_map/add | solution.py:101
  27.0 1.9 %collective-permute-start.6 = (f32[16,3,256]{2,0,1:T(8,128)S(1)}, f32[16,3,256]{2,0,1:T(8,128)S(1)}, u32[]{:S(2)}, u32[]{:S(2)}) collective-permute-start(f32[16,3,256]{2,0,1:T(8,128)S(1)} %get-tuple-element.41), channel_id=1, source_target_pairs={{0,1},{1,2},{2,3},{3,4},{4,5},{5,6},{6,7},{8,9},{9,10},{10,11},{11... | collective-permute-start | bytes 147464 | tf_op jit(solution)/shard_map/ppermute | solution.py:20
  28.9 6.0 %collective-permute-start.7 = (f32[16,3,256]{2,0,1:T(8,128)S(1)}, f32[16,3,256]{2,0,1:T(8,128)S(1)}, u32[]{:S(2)}, u32[]{:S(2)}) collective-permute-start(f32[16,3,256]{2,0,1:T(8,128)S(1)} %get-tuple-element.42), channel_id=1, source_target_pairs={{1,0},{2,1},{3,2},{4,3},{5,4},{6,5},{7,6},{9,8},{10,9},{11,10},{12... | collective-permute-start | bytes 147464 | tf_op jit(solution)/shard_map/ppermute | solution.py:23
  35.1 5.3 %collective-permute-start.5 = (f32[3,32,256]{2,0,1:T(4,128)S(1)}, f32[3,32,256]{2,0,1:T(4,128)S(1)}, u32[]{:S(2)}, u32[]{:S(2)}) collective-permute-start(f32[3,32,256]{2,0,1:T(4,128)S(1)} %get-tuple-element.38), channel_id=1, source_target_pairs={{8,0},{16,8},{24,16},{32,24},{40,32},{48,40},{56,48},{64,56},{72,6... | collective-permute-start | bytes 294920 | tf_op jit(solution)/shard_map/ppermute | solution.py:23
  43.3 8.1 %multiply_add_fusion.4 = f32[16,32,256]{2,0,1:T(8,128)S(1)} fusion(f32[16,32,256]{2,0,1:T(8,128)S(1)} %multiply_add_fusion.5, f32[16,32,261]{2,0,1:T(8,128)S(1)} %slice_subtract_fusion.8, f32[16,37,256]{2,0,1:T(8,128)S(1)} %slice_subtract_fusion.16, f32[21,32,256]{2,0,1:T(8,128)S(1)} %slice_subtract_fusion.9, f32[16,32,256]{2,1,0:T(8,128)S(1)} %copy-done), kind=kLoop, calls=%fused_computation.46 | loop fusion | flops 54919168 | bytes 11010048 | tf_op jit(solution)/shard_map/add | solution.py:102
  51.5 1.9 %collective-permute-start.10 = (f32[16,3,256]{2,0,1:T(8,128)S(1)}, f32[16,3,256]{2,0,1:T(8,128)S(1)}, u32[]{:S(2)}, u32[]{:S(2)}) collective-permute-start(f32[16,3,256]{2,0,1:T(8,128)S(1)} %get-tuple-element.33), channel_id=1, source_target_pairs={{0,1},{1,2},{2,3},{3,4},{4,5},{5,6},{6,7},{8,9},{9,10},{10,11},{11... | collective-permute-start | bytes 147464 | tf_op jit(solution)/shard_map/ppermute | solution.py:20
  53.5 6.0 %collective-permute-start.11 = (f32[16,3,256]{2,0,1:T(8,128)S(1)}, f32[16,3,256]{2,0,1:T(8,128)S(1)}, u32[]{:S(2)}, u32[]{:S(2)}) collective-permute-start(f32[16,3,256]{2,0,1:T(8,128)S(1)} %get-tuple-element.34), channel_id=1, source_target_pairs={{1,0},{2,1},{3,2},{4,3},{5,4},{6,5},{7,6},{9,8},{10,9},{11,10},{12... | collective-permute-start | bytes 147464 | tf_op jit(solution)/shard_map/ppermute | solution.py:23
  59.6 5.3 %collective-permute-start.9 = (f32[3,32,256]{2,0,1:T(4,128)S(1)}, f32[3,32,256]{2,0,1:T(4,128)S(1)}, u32[]{:S(2)}, u32[]{:S(2)}) collective-permute-start(f32[3,32,256]{2,0,1:T(4,128)S(1)} %get-tuple-element.30), channel_id=1, source_target_pairs={{8,0},{16,8},{24,16},{32,24},{40,32},{48,40},{56,48},{64,56},{72,6... | collective-permute-start | bytes 294920 | tf_op jit(solution)/shard_map/ppermute | solution.py:23
  67.8 8.1 %multiply_add_fusion.3 = f32[16,32,256]{2,0,1:T(8,128)S(1)} fusion(f32[16,32,256]{2,0,1:T(8,128)S(1)} %multiply_add_fusion.4, f32[16,32,261]{2,0,1:T(8,128)S(1)} %slice_subtract_fusion.6, f32[16,37,256]{2,0,1:T(8,128)S(1)} %slice_subtract_fusion.15, f32[21,32,256]{2,0,1:T(8,128)S(1)} %slice_subtract_fusion.7, f32[16,32,256]{2,1,0:T(8,128)S(1)} %copy-done), kind=kLoop, calls=%fused_computation.45 | loop fusion | flops 54919168 | bytes 11010048 | tf_op jit(solution)/shard_map/add | solution.py:103
  76.1 1.9 %collective-permute-start.14 = (f32[16,3,256]{2,0,1:T(8,128)S(1)}, f32[16,3,256]{2,0,1:T(8,128)S(1)}, u32[]{:S(2)}, u32[]{:S(2)}) collective-permute-start(f32[16,3,256]{2,0,1:T(8,128)S(1)} %get-tuple-element.25), channel_id=1, source_target_pairs={{0,1},{1,2},{2,3},{3,4},{4,5},{5,6},{6,7},{8,9},{9,10},{10,11},{11... | collective-permute-start | bytes 147464 | tf_op jit(solution)/shard_map/ppermute | solution.py:20
  78.0 6.0 %collective-permute-start.15 = (f32[16,3,256]{2,0,1:T(8,128)S(1)}, f32[16,3,256]{2,0,1:T(8,128)S(1)}, u32[]{:S(2)}, u32[]{:S(2)}) collective-permute-start(f32[16,3,256]{2,0,1:T(8,128)S(1)} %get-tuple-element.26), channel_id=1, source_target_pairs={{1,0},{2,1},{3,2},{4,3},{5,4},{6,5},{7,6},{9,8},{10,9},{11,10},{12... | collective-permute-start | bytes 147464 | tf_op jit(solution)/shard_map/ppermute | solution.py:23
  84.1 5.3 %collective-permute-start.13 = (f32[3,32,256]{2,0,1:T(4,128)S(1)}, f32[3,32,256]{2,0,1:T(4,128)S(1)}, u32[]{:S(2)}, u32[]{:S(2)}) collective-permute-start(f32[3,32,256]{2,0,1:T(4,128)S(1)} %get-tuple-element.22), channel_id=1, source_target_pairs={{8,0},{16,8},{24,16},{32,24},{40,32},{48,40},{56,48},{64,56},{72,6... | collective-permute-start | bytes 294920 | tf_op jit(solution)/shard_map/ppermute | solution.py:23
  92.3 8.0 %multiply_add_fusion.2 = f32[16,32,256]{2,0,1:T(8,128)S(1)} fusion(f32[16,32,256]{2,0,1:T(8,128)S(1)} %multiply_add_fusion.3, f32[16,32,261]{2,0,1:T(8,128)S(1)} %slice_subtract_fusion.4, f32[16,37,256]{2,0,1:T(8,128)S(1)} %slice_subtract_fusion.14, f32[21,32,256]{2,0,1:T(8,128)S(1)} %slice_subtract_fusion.5, f32[16,32,256]{2,1,0:T(8,128)S(1)} %copy-done), kind=kLoop, calls=%fused_computation.44 | loop fusion | flops 54525952 | bytes 11010048 | tf_op jit(solution)/shard_map/add | solution.py:101
  100.6 1.9 %collective-permute-start.18 = (f32[16,3,256]{2,0,1:T(8,128)S(1)}, f32[16,3,256]{2,0,1:T(8,128)S(1)}, u32[]{:S(2)}, u32[]{:S(2)}) collective-permute-start(f32[16,3,256]{2,0,1:T(8,128)S(1)} %get-tuple-element.17), channel_id=1, source_target_pairs={{0,1},{1,2},{2,3},{3,4},{4,5},{5,6},{6,7},{8,9},{9,10},{10,11},{11... | collective-permute-start | bytes 147464 | tf_op jit(solution)/shard_map/ppermute | solution.py:20
  102.5 6.0 %collective-permute-start.19 = (f32[16,3,256]{2,0,1:T(8,128)S(1)}, f32[16,3,256]{2,0,1:T(8,128)S(1)}, u32[]{:S(2)}, u32[]{:S(2)}) collective-permute-start(f32[16,3,256]{2,0,1:T(8,128)S(1)} %get-tuple-element.18), channel_id=1, source_target_pairs={{1,0},{2,1},{3,2},{4,3},{5,4},{6,5},{7,6},{9,8},{10,9},{11,10},{12... | collective-permute-start | bytes 147464 | tf_op jit(solution)/shard_map/ppermute | solution.py:23
  108.6 5.3 %collective-permute-start.17 = (f32[3,32,256]{2,0,1:T(4,128)S(1)}, f32[3,32,256]{2,0,1:T(4,128)S(1)}, u32[]{:S(2)}, u32[]{:S(2)}) collective-permute-start(f32[3,32,256]{2,0,1:T(4,128)S(1)} %get-tuple-element.14), channel_id=1, source_target_pairs={{8,0},{16,8},{24,16},{32,24},{40,32},{48,40},{56,48},{64,56},{72,6... | collective-permute-start | bytes 294920 | tf_op jit(solution)/shard_map/ppermute | solution.py:23
  116.8 8.1 %multiply_add_fusion.1 = f32[16,32,256]{2,0,1:T(8,128)S(1)} fusion(f32[16,32,256]{2,0,1:T(8,128)S(1)} %multiply_add_fusion.2, f32[16,32,261]{2,0,1:T(8,128)S(1)} %slice_subtract_fusion.2, f32[16,37,256]{2,0,1:T(8,128)S(1)} %slice_subtract_fusion.13, f32[21,32,256]{2,0,1:T(8,128)S(1)} %slice_subtract_fusion.3, f32[16,32,256]{2,0,1:T(8,128)S(1)} %multiply_add_fusion.3, ...), kind=kLoop, calls=%fused_computation.43 | loop fusion | flops 54919168 | bytes 11534336 | tf_op jit(solution)/shard_map/add | solution.py:102
  125.1 1.9 %collective-permute-start.22 = (f32[16,3,256]{2,0,1:T(8,128)S(1)}, f32[16,3,256]{2,0,1:T(8,128)S(1)}, u32[]{:S(2)}, u32[]{:S(2)}) collective-permute-start(f32[16,3,256]{2,0,1:T(8,128)S(1)} %get-tuple-element.9), channel_id=1, source_target_pairs={{0,1},{1,2},{2,3},{3,4},{4,5},{5,6},{6,7},{8,9},{9,10},{10,11},{11... | collective-permute-start | bytes 147464 | tf_op jit(solution)/shard_map/ppermute | solution.py:20
  127.0 6.0 %collective-permute-start.23 = (f32[16,3,256]{2,0,1:T(8,128)S(1)}, f32[16,3,256]{2,0,1:T(8,128)S(1)}, u32[]{:S(2)}, u32[]{:S(2)}) collective-permute-start(f32[16,3,256]{2,0,1:T(8,128)S(1)} %get-tuple-element.10), channel_id=1, source_target_pairs={{1,0},{2,1},{3,2},{4,3},{5,4},{6,5},{7,6},{9,8},{10,9},{11,10},{12... | collective-permute-start | bytes 147464 | tf_op jit(solution)/shard_map/ppermute | solution.py:23
  133.2 5.3 %collective-permute-start.21 = (f32[3,32,256]{2,0,1:T(4,128)S(1)}, f32[3,32,256]{2,0,1:T(4,128)S(1)}, u32[]{:S(2)}, u32[]{:S(2)}) collective-permute-start(f32[3,32,256]{2,0,1:T(4,128)S(1)} %get-tuple-element.6), channel_id=1, source_target_pairs={{8,0},{16,8},{24,16},{32,24},{40,32},{48,40},{56,48},{64,56},{72,6... | collective-permute-start | bytes 294920 | tf_op jit(solution)/shard_map/ppermute | solution.py:23
  141.4 8.1 %multiply_add_fusion = f32[16,32,256]{2,0,1:T(8,128)S(1)} fusion(f32[16,32,256]{2,0,1:T(8,128)S(1)} %multiply_add_fusion.1, f32[16,32,261]{2,0,1:T(8,128)S(1)} %slice_subtract_fusion, f32[16,37,256]{2,0,1:T(8,128)S(1)} %slice_subtract_fusion.12, f32[21,32,256]{2,0,1:T(8,128)S(1)} %slice_subtract_fusion.1, f32[16,32,256]{2,0,1:T(8,128)S(1)} %multiply_add_fusion.3, ...), kind=kLoop, calls=%fused_computation.42 | loop fusion | flops 54919168 | bytes 11534336 | tf_op jit(solution)/shard_map/add | solution.py:103
  (119 shorter events, 20.5 us)
Async XLA Ops:
  1.4 16.2 %collective-permute-start.2 = (f32[16,3,256]{2,0,1:T(8,128)S(1)}, f32[16,3,256]{2,0,1:T(8,128)S(1)}, u32[]{:S(2)}, u32[]{:S(2)}) collective-permute-start(f32[16,3,256]{2,0,1:T(8,128)S(1)} %get-tuple-element.49), channel_id=1, source_target_pairs={{0,1},{1,2},{2,3},{3,4},{4,5},{5,6},{6,7},{8,9},{9,10},{10,11},{11... | collective-permute-start | bytes 147464 | tf_op jit(solution)/shard_map/ppermute | solution.py:20
  5.0 12.6 %collective-permute-start.3 = (f32[16,3,256]{2,0,1:T(8,128)S(1)}, f32[16,3,256]{2,0,1:T(8,128)S(1)}, u32[]{:S(2)}, u32[]{:S(2)}) collective-permute-start(f32[16,3,256]{2,0,1:T(8,128)S(1)} %get-tuple-element.50), channel_id=1, source_target_pairs={{1,0},{2,1},{3,2},{4,3},{5,4},{6,5},{7,6},{9,8},{10,9},{11,10},{12... | collective-permute-start | bytes 147464 | tf_op jit(solution)/shard_map/ppermute | solution.py:23
  9.5 9.0 %collective-permute-start = (f32[3,32,256]{2,0,1:T(4,128)S(1)}, f32[3,32,256]{2,0,1:T(4,128)S(1)}, u32[]{:S(2)}, u32[]{:S(2)}) collective-permute-start(f32[3,32,256]{2,0,1:T(4,128)S(1)} %get-tuple-element.45), channel_id=1, source_target_pairs={{0,8},{8,16},{16,24},{24,32},{32,40},{40,48},{48,56},{56,64},{64,7... | collective-permute-start | bytes 294920 | tf_op jit(solution)/shard_map/ppermute | solution.py:20
  9.6 8.9 %collective-permute-start.1 = (f32[3,32,256]{2,0,1:T(4,128)S(1)}, f32[3,32,256]{2,0,1:T(4,128)S(1)}, u32[]{:S(2)}, u32[]{:S(2)}) collective-permute-start(f32[3,32,256]{2,0,1:T(4,128)S(1)} %get-tuple-element.46), channel_id=1, source_target_pairs={{8,0},{16,8},{24,16},{32,24},{40,32},{48,40},{56,48},{64,56},{72,6... | collective-permute-start | bytes 294920 | tf_op jit(solution)/shard_map/ppermute | solution.py:23
  27.0 14.8 %collective-permute-start.6 = (f32[16,3,256]{2,0,1:T(8,128)S(1)}, f32[16,3,256]{2,0,1:T(8,128)S(1)}, u32[]{:S(2)}, u32[]{:S(2)}) collective-permute-start(f32[16,3,256]{2,0,1:T(8,128)S(1)} %get-tuple-element.41), channel_id=1, source_target_pairs={{0,1},{1,2},{2,3},{3,4},{4,5},{5,6},{6,7},{8,9},{9,10},{10,11},{11... | collective-permute-start | bytes 147464 | tf_op jit(solution)/shard_map/ppermute | solution.py:20
  28.9 12.9 %collective-permute-start.7 = (f32[16,3,256]{2,0,1:T(8,128)S(1)}, f32[16,3,256]{2,0,1:T(8,128)S(1)}, u32[]{:S(2)}, u32[]{:S(2)}) collective-permute-start(f32[16,3,256]{2,0,1:T(8,128)S(1)} %get-tuple-element.42), channel_id=1, source_target_pairs={{1,0},{2,1},{3,2},{4,3},{5,4},{6,5},{7,6},{9,8},{10,9},{11,10},{12... | collective-permute-start | bytes 147464 | tf_op jit(solution)/shard_map/ppermute | solution.py:23
  35.0 8.1 %collective-permute-start.4 = (f32[3,32,256]{2,0,1:T(4,128)S(1)}, f32[3,32,256]{2,0,1:T(4,128)S(1)}, u32[]{:S(2)}, u32[]{:S(2)}) collective-permute-start(f32[3,32,256]{2,0,1:T(4,128)S(1)} %get-tuple-element.37), channel_id=1, source_target_pairs={{0,8},{8,16},{16,24},{24,32},{32,40},{40,48},{48,56},{56,64},{64,7... | collective-permute-start | bytes 294920 | tf_op jit(solution)/shard_map/ppermute | solution.py:20
  35.1 8.0 %collective-permute-start.5 = (f32[3,32,256]{2,0,1:T(4,128)S(1)}, f32[3,32,256]{2,0,1:T(4,128)S(1)}, u32[]{:S(2)}, u32[]{:S(2)}) collective-permute-start(f32[3,32,256]{2,0,1:T(4,128)S(1)} %get-tuple-element.38), channel_id=1, source_target_pairs={{8,0},{16,8},{24,16},{32,24},{40,32},{48,40},{56,48},{64,56},{72,6... | collective-permute-start | bytes 294920 | tf_op jit(solution)/shard_map/ppermute | solution.py:23
  51.5 14.8 %collective-permute-start.10 = (f32[16,3,256]{2,0,1:T(8,128)S(1)}, f32[16,3,256]{2,0,1:T(8,128)S(1)}, u32[]{:S(2)}, u32[]{:S(2)}) collective-permute-start(f32[16,3,256]{2,0,1:T(8,128)S(1)} %get-tuple-element.33), channel_id=1, source_target_pairs={{0,1},{1,2},{2,3},{3,4},{4,5},{5,6},{6,7},{8,9},{9,10},{10,11},{11... | collective-permute-start | bytes 147464 | tf_op jit(solution)/shard_map/ppermute | solution.py:20
  53.5 12.9 %collective-permute-start.11 = (f32[16,3,256]{2,0,1:T(8,128)S(1)}, f32[16,3,256]{2,0,1:T(8,128)S(1)}, u32[]{:S(2)}, u32[]{:S(2)}) collective-permute-start(f32[16,3,256]{2,0,1:T(8,128)S(1)} %get-tuple-element.34), channel_id=1, source_target_pairs={{1,0},{2,1},{3,2},{4,3},{5,4},{6,5},{7,6},{9,8},{10,9},{11,10},{12... | collective-permute-start | bytes 147464 | tf_op jit(solution)/shard_map/ppermute | solution.py:23
  59.5 8.1 %collective-permute-start.8 = (f32[3,32,256]{2,0,1:T(4,128)S(1)}, f32[3,32,256]{2,0,1:T(4,128)S(1)}, u32[]{:S(2)}, u32[]{:S(2)}) collective-permute-start(f32[3,32,256]{2,0,1:T(4,128)S(1)} %get-tuple-element.29), channel_id=1, source_target_pairs={{0,8},{8,16},{16,24},{24,32},{32,40},{40,48},{48,56},{56,64},{64,7... | collective-permute-start | bytes 294920 | tf_op jit(solution)/shard_map/ppermute | solution.py:20
  59.6 8.0 %collective-permute-start.9 = (f32[3,32,256]{2,0,1:T(4,128)S(1)}, f32[3,32,256]{2,0,1:T(4,128)S(1)}, u32[]{:S(2)}, u32[]{:S(2)}) collective-permute-start(f32[3,32,256]{2,0,1:T(4,128)S(1)} %get-tuple-element.30), channel_id=1, source_target_pairs={{8,0},{16,8},{24,16},{32,24},{40,32},{48,40},{56,48},{64,56},{72,6... | collective-permute-start | bytes 294920 | tf_op jit(solution)/shard_map/ppermute | solution.py:23
  76.1 14.8 %collective-permute-start.14 = (f32[16,3,256]{2,0,1:T(8,128)S(1)}, f32[16,3,256]{2,0,1:T(8,128)S(1)}, u32[]{:S(2)}, u32[]{:S(2)}) collective-permute-start(f32[16,3,256]{2,0,1:T(8,128)S(1)} %get-tuple-element.25), channel_id=1, source_target_pairs={{0,1},{1,2},{2,3},{3,4},{4,5},{5,6},{6,7},{8,9},{9,10},{10,11},{11... | collective-permute-start | bytes 147464 | tf_op jit(solution)/shard_map/ppermute | solution.py:20
  78.0 12.9 %collective-permute-start.15 = (f32[16,3,256]{2,0,1:T(8,128)S(1)}, f32[16,3,256]{2,0,1:T(8,128)S(1)}, u32[]{:S(2)}, u32[]{:S(2)}) collective-permute-start(f32[16,3,256]{2,0,1:T(8,128)S(1)} %get-tuple-element.26), channel_id=1, source_target_pairs={{1,0},{2,1},{3,2},{4,3},{5,4},{6,5},{7,6},{9,8},{10,9},{11,10},{12... | collective-permute-start | bytes 147464 | tf_op jit(solution)/shard_map/ppermute | solution.py:23
  84.0 8.1 %collective-permute-start.12 = (f32[3,32,256]{2,0,1:T(4,128)S(1)}, f32[3,32,256]{2,0,1:T(4,128)S(1)}, u32[]{:S(2)}, u32[]{:S(2)}) collective-permute-start(f32[3,32,256]{2,0,1:T(4,128)S(1)} %get-tuple-element.21), channel_id=1, source_target_pairs={{0,8},{8,16},{16,24},{24,32},{32,40},{40,48},{48,56},{56,64},{64,7... | collective-permute-start | bytes 294920 | tf_op jit(solution)/shard_map/ppermute | solution.py:20
  84.1 8.0 %collective-permute-start.13 = (f32[3,32,256]{2,0,1:T(4,128)S(1)}, f32[3,32,256]{2,0,1:T(4,128)S(1)}, u32[]{:S(2)}, u32[]{:S(2)}) collective-permute-start(f32[3,32,256]{2,0,1:T(4,128)S(1)} %get-tuple-element.22), channel_id=1, source_target_pairs={{8,0},{16,8},{24,16},{32,24},{40,32},{48,40},{56,48},{64,56},{72,6... | collective-permute-start | bytes 294920 | tf_op jit(solution)/shard_map/ppermute | solution.py:23
  100.6 14.8 %collective-permute-start.18 = (f32[16,3,256]{2,0,1:T(8,128)S(1)}, f32[16,3,256]{2,0,1:T(8,128)S(1)}, u32[]{:S(2)}, u32[]{:S(2)}) collective-permute-start(f32[16,3,256]{2,0,1:T(8,128)S(1)} %get-tuple-element.17), channel_id=1, source_target_pairs={{0,1},{1,2},{2,3},{3,4},{4,5},{5,6},{6,7},{8,9},{9,10},{10,11},{11... | collective-permute-start | bytes 147464 | tf_op jit(solution)/shard_map/ppermute | solution.py:20
  102.5 12.9 %collective-permute-start.19 = (f32[16,3,256]{2,0,1:T(8,128)S(1)}, f32[16,3,256]{2,0,1:T(8,128)S(1)}, u32[]{:S(2)}, u32[]{:S(2)}) collective-permute-start(f32[16,3,256]{2,0,1:T(8,128)S(1)} %get-tuple-element.18), channel_id=1, source_target_pairs={{1,0},{2,1},{3,2},{4,3},{5,4},{6,5},{7,6},{9,8},{10,9},{11,10},{12... | collective-permute-start | bytes 147464 | tf_op jit(solution)/shard_map/ppermute | solution.py:23
  108.5 8.1 %collective-permute-start.16 = (f32[3,32,256]{2,0,1:T(4,128)S(1)}, f32[3,32,256]{2,0,1:T(4,128)S(1)}, u32[]{:S(2)}, u32[]{:S(2)}) collective-permute-start(f32[3,32,256]{2,0,1:T(4,128)S(1)} %get-tuple-element.13), channel_id=1, source_target_pairs={{0,8},{8,16},{16,24},{24,32},{32,40},{40,48},{48,56},{56,64},{64,7... | collective-permute-start | bytes 294920 | tf_op jit(solution)/shard_map/ppermute | solution.py:20
  108.6 8.0 %collective-permute-start.17 = (f32[3,32,256]{2,0,1:T(4,128)S(1)}, f32[3,32,256]{2,0,1:T(4,128)S(1)}, u32[]{:S(2)}, u32[]{:S(2)}) collective-permute-start(f32[3,32,256]{2,0,1:T(4,128)S(1)} %get-tuple-element.14), channel_id=1, source_target_pairs={{8,0},{16,8},{24,16},{32,24},{40,32},{48,40},{56,48},{64,56},{72,6... | collective-permute-start | bytes 294920 | tf_op jit(solution)/shard_map/ppermute | solution.py:23
  125.1 14.8 %collective-permute-start.22 = (f32[16,3,256]{2,0,1:T(8,128)S(1)}, f32[16,3,256]{2,0,1:T(8,128)S(1)}, u32[]{:S(2)}, u32[]{:S(2)}) collective-permute-start(f32[16,3,256]{2,0,1:T(8,128)S(1)} %get-tuple-element.9), channel_id=1, source_target_pairs={{0,1},{1,2},{2,3},{3,4},{4,5},{5,6},{6,7},{8,9},{9,10},{10,11},{11... | collective-permute-start | bytes 147464 | tf_op jit(solution)/shard_map/ppermute | solution.py:20
  127.0 12.9 %collective-permute-start.23 = (f32[16,3,256]{2,0,1:T(8,128)S(1)}, f32[16,3,256]{2,0,1:T(8,128)S(1)}, u32[]{:S(2)}, u32[]{:S(2)}) collective-permute-start(f32[16,3,256]{2,0,1:T(8,128)S(1)} %get-tuple-element.10), channel_id=1, source_target_pairs={{1,0},{2,1},{3,2},{4,3},{5,4},{6,5},{7,6},{9,8},{10,9},{11,10},{12... | collective-permute-start | bytes 147464 | tf_op jit(solution)/shard_map/ppermute | solution.py:23
  133.1 8.1 %collective-permute-start.20 = (f32[3,32,256]{2,0,1:T(4,128)S(1)}, f32[3,32,256]{2,0,1:T(4,128)S(1)}, u32[]{:S(2)}, u32[]{:S(2)}) collective-permute-start(f32[3,32,256]{2,0,1:T(4,128)S(1)} %get-tuple-element.5), channel_id=1, source_target_pairs={{0,8},{8,16},{16,24},{24,32},{32,40},{40,48},{48,56},{56,64},{64,7... | collective-permute-start | bytes 294920 | tf_op jit(solution)/shard_map/ppermute | solution.py:20
  133.2 8.0 %collective-permute-start.21 = (f32[3,32,256]{2,0,1:T(4,128)S(1)}, f32[3,32,256]{2,0,1:T(4,128)S(1)}, u32[]{:S(2)}, u32[]{:S(2)}) collective-permute-start(f32[3,32,256]{2,0,1:T(4,128)S(1)} %get-tuple-element.6), channel_id=1, source_target_pairs={{8,0},{16,8},{24,16},{32,24},{40,32},{48,40},{56,48},{64,56},{72,6... | collective-permute-start | bytes 294920 | tf_op jit(solution)/shard_map/ppermute | solution.py:23
  (1 other events, 14.7 us)
where the time goes:
time: 151 us
  starting transfers between devices  81.4 us (54%)
  other arithmetic  54.3 us (36%)
  local copies, waits for them, and re-layouts  8.26 us (5%)
  waiting for transfers between devices  5.72 us (4%)
    ppermute x12, starting transfers between devices, padded_2(): lax.ppermute(lax.slice_in_dim(block, 0, width, axis=dim), axis, backward)  67.7 us
    add x2, other arithmetic, per_device(): 1.0 / 3.0 * field  16.1 us
    add x2, other arithmetic, per_device(): 0.75 * field + 0.25 * (first + pseudo_step * section_rate(first, sign))  16.1 us
    add x2, other arithmetic, per_device(): first = field + pseudo_step * section_rate(field, sign)  16 us
    ppermute x12, starting transfers between devices, padded_2(): lax.ppermute(lax.slice_in_dim(block, block.shape[dim] - width, None, axis...  13.7 us
    ppermute x12, waiting for transfers between devices, padded_2(): lax.ppermute(lax.slice_in_dim(block, block.shape[dim] - width, None, axis...  5.69 us
    slice x18, local copies, waits for them, and re-layouts, rate(): x_ext = jnp.pad(center, ((0, 0), (0, 0), (3, 3)), mode='edge')  3.8 us
  transfers between devices with their start and end apart: 24, of which 6 were waited for; matrix products, arithmetic and copies ran while one was open for 6% of the time, Pallas kernels for 0%

commit v1 on v0

v1 whole, which is shorter than its diff:
```python
import functools

import jax
import jax.numpy as jnp
from jax import lax
from jax.experimental import pallas as pl
from jax.experimental.pallas import tpu as pltpu
from jax.sharding import PartitionSpec as P

STEPS = 2
TAU = 0.3
EPS = 0.75e-6

DEEP = 9
PITCH = 64
ROW0 = 16
f32 = jnp.float32


def triple(g, h, curve):
    lean = 1.5 * curve
    mid = curve * curve + (0.75 * (g * h) + EPS)
    left = mid + lean * h
    right = mid - lean * g
    return left * left, mid * mid, right * right


def face(a, b, c, jump_low, jump_high, base_back, base_fore):
    p = b * c
    q = a * c
    r = a * b
    half = 0.5 * (p + r) + 3.0 * q
    pj = p * jump_low
    rj = r * jump_high
    back = base_back - (pj + 1.5 * rj) / (half + r)
    fore = base_fore - (1.5 * pj + rj) / (half + p)
    return back, fore


def upwind(back, fore, side):
    best = jnp.maximum(jnp.maximum(side * back, side * fore), 0.0)
    return best * best


def bases(center, low_slope, high_slope):
    six = 6.0 * center
    both = low_slope + high_slope
    return six + (both + high_slope), (both + low_slope) - six


def at(z, r, n=8):
    return pl.ds(z * PITCH + r, n)


def z_pass(src, side, acc, margin, tiles):
    first = DEEP - margin
    last = DEEP + 16 + margin
    r0 = ROW0 - margin

    def column(t, carry):
        r = r0 + 8 * t
        state = [dict(), dict()]
        for k in range(first - 1, last):
            for h in range(2):
                s = state[h]

                def u(z):
                    if ("u", z) not in s:
                        s["u", z] = src[h, at(z, r), :]
                    return s["u", z]

                def d(z):
                    if ("d", z) not in s:
                        s["d", z] = u(z + 1) - u(z)
                    return s["d", z]

                def e(z):
                    if ("e", z) not in s:
                        s["e", z] = d(z + 1) - d(z)
                    return s["e", z]

                def c(z):
                    if ("c", z) not in s:
                        s["c", z] = e(z) - e(z - 1)
                    return s["c", z]

                def j(z):
                    if ("j", z) not in s:
                        s["j", z] = c(z) - c(z - 1)
                    return s["j", z]

                def tr(z):
                    if ("t", z) not in s:
                        s["t", z] = triple(e(z - 1), e(z), c(z))
                    return s["t", z]

                base_back, base_fore = bases(d(k), e(k - 1), e(k))
                back, fore = face(
                    tr(k - 1)[0], tr(k)[1], tr(k + 1)[2], j(k), j(k + 1), base_back, base_fore
                )
                if k >= first:
                    acc[h, pl.ds((k - first) * 48 + 8 * t, 8), :] = upwind(
                        s["back"], fore, side[h, at(k, r), :]
                    )
                s["back"] = back
        return carry

    lax.fori_loop(0, tiles, column, 0)


def y_pass(src, side, acc, scr, margin, tiles, face_tiles, triple_tiles, planes_at_once):
    first = DEEP - margin
    count = 16 + 2 * margin
    r0 = ROW0 - margin
    left_s, mid_s, right_s, curve_s, diff_s, fore_s = scr

    def plane(i, carry):
        for sub in range(planes_at_once):
            zi = i * planes_at_once + sub
            z = first + zi
            for h in range(2):
                slot = sub * 2 + h
                for t in range(triple_tiles):
                    r = r0 - 2 + 8 * t
                    u0 = src[h, at(z, r - 1), :]
                    u1 = src[h, at(z, r), :]
                    u2 = src[h, at(z, r + 1), :]
                    u3 = src[h, at(z, r + 2), :]
                    d1 = u2 - u1
                    g = d1 - (u1 - u0)
                    e = (u3 - u2) - d1
                    curve = e - g
                    rows = pl.ds(8 * t, 8)
                    left_s[slot, rows, :], mid_s[slot, rows, :], right_s[slot, rows, :] = triple(g, e, curve)
                    curve_s[slot, rows, :] = curve
                    diff_s[slot, rows, :] = d1
            for h in range(2):
                slot = sub * 2 + h
                backs = []
                for t in range(face_tiles):
                    lo, me, hi = pl.ds(8 * t, 8), pl.ds(8 * t + 1, 8), pl.ds(8 * t + 2, 8)
                    dl, dm, dh = diff_s[slot, lo, :], diff_s[slot, me, :], diff_s[slot, hi, :]
                    cm = curve_s[slot, me, :]
                    back, fore = face(
                        left_s[slot, lo, :],
                        mid_s[slot, me, :],
                        right_s[slot, hi, :],
                        cm - curve_s[slot, lo, :],
                        curve_s[slot, hi, :] - cm,
                        5.0 * dm + ((dh + dh) - dl),
                        (dh - (dl + dl)) - 5.0 * dm,
                    )
                    fore_s[slot, pl.ds(8 * t, 8), :] = fore
                    backs.append(back)
                for t in range(tiles):
                    fore = fore_s[slot, pl.ds(8 * t + 1, 8), :]
                    rows = pl.ds(zi * 48 + 8 * t, 8)
                    acc[h, rows, :] += upwind(backs[t], fore, side[h, at(z, r0 + 8 * t), :])
        return carry

    lax.fori_loop(0, count // planes_at_once, plane, 0)


def x_pass(src, side, rate_of, acc, put, scr, margin, tiles, combine):
    first = DEEP - margin
    count = 16 + 2 * margin
    r0 = ROW0 - margin
    lane = lax.broadcasted_iota(jnp.int32, (8, 128), 1)
    below_last = lane < 127
    below_two = lane < 126
    above_first = lane > 0
    shifted, finished = (scr[0], scr[1]), (scr[2], scr[3])

    def shift(z, out):
        for t in range(tiles):
            even, odd = src[0, at(z, r0 + 8 * t), :], src[1, at(z, r0 + 8 * t), :]
            rows = pl.ds(8 * t, 8)
            out[0, rows, :] = jnp.where(above_first, pltpu.roll(even, 1, 1), even)
            out[1, rows, :] = jnp.where(above_first, pltpu.roll(odd, 1, 1), even)
            out[2, rows, :] = jnp.where(below_last, pltpu.roll(even, 127, 1), odd)
            odd_up = jnp.where(below_last, pltpu.roll(odd, 127, 1), odd)
            out[3, rows, :] = odd_up
            out[4, rows, :] = jnp.where(below_two, pltpu.roll(even, 126, 1), odd_up)

    def finish(h, zi, t, back, fore):
        z = first + zi
        r = r0 + 8 * t
        total = acc[h, pl.ds(zi * 48 + 8 * t, 8), :] + upwind(back, fore, side[h, at(z, r), :])
        norm = total * lax.rsqrt(jnp.maximum(total, 1e-30))
        stepped = src[h, at(z, r), :] + rate_of[h, at(z, r), :] * ((1.0 / 6.0) * norm - 1.0)
        put(h, zi, t, r, combine(h, z, r, stepped))

    def finish_even(zi, done):
        for t in range(tiles):
            rows = pl.ds(8 * t, 8)
            finish(0, zi, t, done[0, rows, :], done[1, rows, :])

    def faces(zi, inp, done):
        z = first + zi
        for t in range(tiles):
            rows = pl.ds(8 * t, 8)
            u = [
                inp[0, rows, :],
                inp[1, rows, :],
                src[0, at(z, r0 + 8 * t), :],
                src[1, at(z, r0 + 8 * t), :],
                inp[2, rows, :],
                inp[3, rows, :],
                inp[4, rows, :],
            ]
            d = [u[i + 1] - u[i] for i in range(6)]
            e = [d[i + 1] - d[i] for i in range(5)]
            c = [e[i + 1] - e[i] for i in range(4)]
            jump = [c[i + 1] - c[i] for i in range(3)]
            tri = [triple(e[i], e[i + 1], c[i]) for i in range(4)]
            back_even, fore_even = face(
                tri[0][0], tri[1][1], tri[2][2], jump[0], jump[1], *bases(d[2], e[1], e[2])
            )
            back_odd, fore_odd = face(
                tri[1][0], tri[2][1], tri[3][2], jump[1], jump[2], *bases(d[3], e[2], e[3])
            )
            edge, _ = face(EPS * EPS, tri[0][1], tri[1][2], c[0], jump[0], e[1] + e[1], e[1])
            done[0, rows, :] = jnp.where(above_first, pltpu.roll(back_odd, 1, 1), edge)
            done[1, rows, :] = fore_even
            finish(1, zi, t, back_even, fore_odd)

    shift(first, shifted[0])

    def two_planes(i, carry):
        zi = 2 * i
        shift(first + zi + 1, shifted[1])
        finish_even(jnp.maximum(zi - 1, 0), finished[1])
        faces(zi, shifted[0], finished[0])
        shift(first + zi + 2, shifted[0])
        finish_even(zi, finished[0])
        faces(zi + 1, shifted[1], finished[1])
        return carry

    lax.fori_loop(0, count // 2, two_planes, 0)
    finish_even(count - 1, finished[1])


def load_block(work, own_ref, zo_ref, ze_ref, yo_ref, ye_ref, odd_z, odd_y, is_first, is_last):
    def planes(ref, start, count):
        def one(k, carry):
            for t in range(4):
                for h in range(2):
                    work[h, at(start + k, ROW0 + 8 * t), :] = ref[k, h, 8 * t : 8 * t + 8, :]
            return carry

        lax.fori_loop(0, count, one, 0)

    planes(own_ref, DEEP, 16)
    planes(zo_ref, 25 * odd_z, DEEP)
    planes(ze_ref, 25 * (1 - odd_z), DEEP)

    def low(ref):
        def one(z, carry):
            for h in range(2):
                work[h, at(z, ROW0 - 8), :] = ref[h, pl.ds(8 * z, 8), :]
                work[h, at(z, ROW0 - 9, 1), :] = ref[h, pl.ds(272 + z, 1), :]
            return carry

        lax.fori_loop(0, 34, one, 0)

    def high(ref):
        def one(z, carry):
            for h in range(2):
                work[h, at(z, ROW0 + 32), :] = ref[h, pl.ds(8 * z, 8), :]
                work[h, at(z, ROW0 + 40, 1), :] = ref[h, pl.ds(272 + z, 1), :]
            return carry

        lax.fori_loop(0, 34, one, 0)

    @pl.when(odd_y == 0)
    def _():
        low(yo_ref)
        high(ye_ref)

    @pl.when(odd_y == 1)
    def _():
        low(ye_ref)
        high(yo_ref)

    edge_rows(work, 0, 34, True, is_first, is_last)


def edge_rows(work, start, count, far, is_first, is_last):
    @pl.when(is_first)
    def _():
        def one(k, carry):
            z = start + k
            for h in range(2):
                row = work[h, at(z, ROW0, 1), :]
                work[h, at(z, ROW0 - 8), :] = jnp.broadcast_to(row, (8, 128))
                if far:
                    work[h, at(z, ROW0 - 9, 1), :] = row
            return carry

        lax.fori_loop(0, count, one, 0)

    @pl.when(is_last)
    def _():
        def one(k, carry):
            z = start + k
            for h in range(2):
                row = work[h, at(z, ROW0 + 31, 1), :]
                work[h, at(z, ROW0 + 32), :] = jnp.broadcast_to(row, (8, 128))
                if far:
                    work[h, at(z, ROW0 + 40, 1), :] = row
            return carry

        lax.fori_loop(0, count, one, 0)


def step_kernel(initial, *refs):
    refs = list(refs)
    own_ref, zo_ref, ze_ref, yo_ref, ye_ref = refs[:5]
    refs = refs[5:]
    if initial:
        out_ref, so_ref, se_ref, keep = refs[:4]
        refs = refs[4:]
        weight = keep
    else:
        weight, out_ref = refs[:2]
        refs = refs[2:]
    u, first, second, side, acc = refs[:5]
    scr = refs[5:11]
    x_scr = refs[11:15]
    third = refs[15]
    gz, gy = lax.axis_index("gz"), lax.axis_index("gy")
    odd_z, odd_y = lax.rem(gz, 2), lax.rem(gy, 2)
    is_first, is_last = gy == 0, gy == lax.axis_size("gy") - 1
    load_block(u, own_ref, zo_ref, ze_ref, yo_ref, ye_ref, odd_z, odd_y, is_first, is_last)

    def signs(k, carry):
        z = 3 + k
        for h in range(2):
            for t in range(6):
                rows = at(z, 10 + 8 * t)
                if initial:
                    v = u[h, rows, :]
                    w = (-TAU) * (v / jnp.sqrt(v * v + 1.0))
                    weight[h, rows, :] = w
                else:
                    w = weight[h, rows, :]
                side[h, rows, :] = jnp.where(w <= 0.0, 1.0, -1.0)
        return carry

    lax.fori_loop(0, 28, signs, 0)

    def store(work, start):
        def put(h, zi, t, r, value):
            work[h, at(start + zi, r), :] = value

        return put

    def put_out(h, zi, t, r, value):
        out_ref[zi, h, 8 * t : 8 * t + 8, :] = value

    def put_third(h, zi, t, r, value):
        third[h, pl.ds(zi * 32 + 8 * t, 8), :] = value

    stages = (
        (u, store(first, 3), 6, 6, 6, 6, lambda h, z, r, v: v),
        (first, store(second, 6), 3, 5, 5, 6, lambda h, z, r, v: 0.75 * u[h, at(z, r), :] + 0.25 * v),
        (
            second,
            put_out if initial else put_third,
            0,
            4,
            5,
            5,
            lambda h, z, r, v: (1.0 / 3.0) * u[h, at(z, r), :] + (2.0 / 3.0) * v,
        ),
    )
    for index, (src, dst, margin, tiles, face_tiles, triple_tiles, combine) in enumerate(stages):
        z_pass(src, side, acc, margin, tiles)
        y_pass(src, side, acc, scr, margin, tiles, face_tiles, triple_tiles, 2)
        x_pass(src, side, weight, acc, dst, x_scr, margin, tiles, combine)
        if index < 2:
            edge_rows((first, second)[index], DEEP - margin, 16 + 2 * margin, False, is_first, is_last)

    if initial:

        def slabs(k, carry):
            so_ref[k] = out_ref[k + 7 * odd_z]
            se_ref[k] = out_ref[k + 7 * (1 - odd_z)]
            return carry

        lax.fori_loop(0, DEEP, slabs, 0)
    else:
        lane = lax.broadcasted_iota(jnp.int32, (8, 128), 1)
        even = (lane & 1) == 0
        half = lane >> 1

        def merge(k, carry):
            for t in range(4):
                rows = pl.ds(k * 32 + 8 * t, 8)
                for h in range(2):
                    parts = [jnp.take_along_axis(third[p, rows, :], half + 64 * h, axis=1) for p in range(2)]
                    out_ref[k, 8 * t : 8 * t + 8, 128 * h : 128 * h + 128] = jnp.where(even, *parts)
            return carry

        lax.fori_loop(0, 16, merge, 0)


def split_kernel(own_ref, out_ref, so_ref, se_ref):
    odd_z = lax.rem(lax.axis_index("gz"), 2)
    lane = lax.broadcasted_iota(jnp.int32, (8, 128), 1)
    low = lane < 64
    twice = (lane & 63) * 2

    def plane(k, carry):
        for t in range(4):
            v = [own_ref[k, 8 * t : 8 * t + 8, 128 * h : 128 * h + 128] for h in range(2)]
            for p in range(2):
                parts = [jnp.take_along_axis(x, twice + p, axis=1) for x in v]
                out_ref[k, p, 8 * t : 8 * t + 8, :] = jnp.where(low, *parts)
        return carry

    lax.fori_loop(0, 16, plane, 0)

    def slabs(k, carry):
        so_ref[k] = out_ref[k + 7 * odd_z]
        se_ref[k] = out_ref[k + 7 * (1 - odd_z)]
        return carry

    lax.fori_loop(0, DEEP, slabs, 0)


def pack_kernel(own_ref, zo_ref, ze_ref, yo_ref, ye_ref):
    odd_z = lax.rem(lax.axis_index("gz"), 2)
    odd_y = lax.rem(lax.axis_index("gy"), 2)

    def fill(out, main, extra):
        def planes(ref, start, count):
            def one(k, carry):
                for h in range(2):
                    out[h, pl.ds(8 * (start + k), 8), :] = ref[k, h, main : main + 8, :]
                    out[h, pl.ds(272 + start + k, 1), :] = ref[k, h, extra : extra + 1, :]
                return carry

            lax.fori_loop(0, count, one, 0)

        planes(own_ref, DEEP, 16)
        planes(zo_ref, 25 * odd_z, DEEP)
        planes(ze_ref, 25 * (1 - odd_z), DEEP)
        out[:, 306:312, :] = jnp.zeros((2, 6, 128), f32)

    @pl.when(odd_y == 0)
    def _():
        fill(yo_ref, 0, 8)
        fill(ye_ref, 24, 23)

    @pl.when(odd_y == 1)
    def _():
        fill(yo_ref, 24, 23)
        fill(ye_ref, 0, 8)


def swaps(count, start, periodic):
    pairs = []
    for low in range(start, count, 2):
        if low + 1 < count or periodic:
            high = (low + 1) % count
            pairs += [(low, high), (high, low)]
    return pairs


VMEM = pl.BlockSpec(memory_space=pltpu.VMEM)
WORK = (2, 34 * PITCH, 128)


def per_device(level_set):
    n_z, n_y = lax.axis_size("gz"), lax.axis_size("gy")
    z_odd, z_even = swaps(n_z, 1, True), swaps(n_z, 0, True)
    y_odd, y_even = swaps(n_y, 1, False), swaps(n_y, 0, False)
    slab = jax.ShapeDtypeStruct((2, 312, 128), f32)
    deep = jax.ShapeDtypeStruct((DEEP, 2, 32, 128), f32)
    split = jax.ShapeDtypeStruct((16, 2, 32, 128), f32)
    params = pltpu.CompilerParams(vmem_limit_bytes=30 * 1024 * 1024)
    pack = pl.pallas_call(
        pack_kernel,
        out_shape=[slab, slab],
        in_specs=[VMEM] * 3,
        out_specs=[VMEM] * 2,
        compiler_params=params,
        name="pack_rows",
    )
    field, z_send_odd, z_send_even = pl.pallas_call(
        split_kernel,
        out_shape=[split, deep, deep],
        in_specs=[VMEM],
        out_specs=[VMEM] * 3,
        compiler_params=params,
        name="split_cells",
    )(level_set)
    keep = None
    for step in range(STEPS):
        zo = lax.ppermute(z_send_odd, "gz", z_odd)
        ze = lax.ppermute(z_send_even, "gz", z_even)
        y_send_odd, y_send_even = pack(field, zo, ze)
        yo = lax.ppermute(y_send_odd, "gy", y_odd)
        ye = lax.ppermute(y_send_even, "gy", y_even)
        initial = step == 0
        block = jax.ShapeDtypeStruct((16, 32, 256), f32)
        work = jax.ShapeDtypeStruct(WORK, f32)
        outs = [split, deep, deep, work] if initial else [block]
        args = (field, zo, ze, yo, ye) + (() if initial else (keep,))
        result = pl.pallas_call(
            functools.partial(step_kernel, initial),
            out_shape=outs,
            in_specs=[VMEM] * len(args),
            out_specs=[VMEM] * len(outs),
            scratch_shapes=[pltpu.VMEM(WORK, f32)] * 4
            + [pltpu.VMEM((2, 28 * 48, 128), f32)]
            + [pltpu.VMEM((4, 56, 128), f32)] * 6
            + [pltpu.VMEM((5, 48, 128), f32)] * 2
            + [pltpu.VMEM((2, 48, 128), f32)] * 2
            + [pltpu.VMEM((2, 512, 128), f32)],
            compiler_params=params,
            name="first_step" if initial else "next_step",
        )(*args)
        if initial:
            field, z_send_odd, z_send_even, keep = result
        else:
            (field,) = result
    return field


def solution(mesh):
    return jax.shard_map(
        per_device,
        mesh=mesh,
        in_specs=(P("gz", "gy", None),),
        out_specs=P("gz", "gy", None),
        check_vma=False,
    )
```

time: 151 us -> 94.7 us (0.63)
  starting transfers between devices: 81.4 us -> 21.5 us
  other arithmetic: 54.3 us -> 0 us
  Pallas kernels: 0 us -> 48.4 us
  waiting for transfers between devices: 5.72 us -> 23.6 us
  local copies, waits for them, and re-layouts: 8.26 us -> 1.04 us
    ppermute x24 -> x8, starting transfers between devices: 81.4 us -> 21.5 us  [the longest x2 11.6 us: per_device(): zo = lax.ppermute(z_send_odd, 'gz', z_odd)]
    pallas_call x0 -> x5, Pallas kernels: none -> 48.4 us  [the longest x2 45.8 us: per_device(): pl.pallas_call(functools.partial(step_kernel, initial), out_shape=outs, i...]
    add x6 -> x0, other arithmetic: 48.3 us -> none  [the longest x2 16.1 us: per_device(): 1.0 / 3.0 * field]
    ppermute x24 -> x8, waiting for transfers between devices: 5.72 us -> 23.6 us  [the longest x2 12.1 us: per_device(): yo = lax.ppermute(y_send_odd, 'gy', y_odd)]
    slice x30 -> x0, local copies, waits for them, and re-layouts: 4.15 us -> none  [the longest x18 3.8 us: rate(): x_ext = jnp.pad(center, ((0, 0), (0, 0), (3, 3)), mode='edge')]
    concatenate x12 -> x0, other arithmetic: 2.73 us -> none  [the longest x6 2.05 us: rate(): x_ext = jnp.pad(center, ((0, 0), (0, 0), (3, 3)), mode='edge')]
    sub x18 -> x0, other arithmetic: 2.41 us -> none  [weno_pair(): diffs = jnp.diff(padded, axis=axis)]
    reshape x12 -> x0, local copies, waits for them, and re-layouts: 1.63 us -> none  [rate(): x_ext = jnp.pad(center, ((0, 0), (0, 0), (3, 3)), mode='edge')]
  transfers between devices with their start and end apart: 24 -> 8, of which waited for: 6 -> 5; matrix products, arithmetic and copies ran while one was open for 6% -> 0% of each run, Pallas kernels for 0% -> 0%
where the time goes in v1:
time: 94.7 us; the launch traced here: 94.5 us
  Pallas kernels  48.4 us (51%)
  waiting for transfers between devices  23.6 us (25%)
  starting transfers between devices  21.5 us (23%)
  local copies, waits for them, and re-layouts  1.04 us (1%)
    pallas_call x2, Pallas kernels, per_device(): pl.pallas_call(functools.partial(step_kernel, initial), out_shape=outs, i...  45.8 us
    ppermute x2, waiting for transfers between devices, per_device(): yo = lax.ppermute(y_send_odd, 'gy', y_odd)  12.1 us
    ppermute x2, starting transfers between devices, per_device(): zo = lax.ppermute(z_send_odd, 'gz', z_odd)  11.6 us
    ppermute x2, starting transfers between devices, per_device(): yo = lax.ppermute(y_send_odd, 'gy', y_odd)  9.7 us
    ppermute x2, waiting for transfers between devices, per_device(): zo = lax.ppermute(z_send_odd, 'gz', z_odd)  9.62 us
  transfers between devices with their start and end apart: 8, of which 5 were waited for; matrix products, arithmetic and copies ran while one was open for 0% of the time, Pallas kernels for 0%

profile of v1, /device:TPU:2, one launch (start us, length us, event | category | flops | bytes accessed | tf_op | source)
XLA Modules:
  0.0 94.5 jit_solution(14488219951800827352)
XLA Ops:
  0.0 0.0 copy-start
  0.0 1.0 %copy-done = f32[16,32,256]{2,1,0:T(8,128)S(1)} copy-done((f32[16,32,256]{2,1,0:T(8,128)S(1)}, f32[16,32,256]{2,1,0:T(8,128)}, u32[]{:S(2)}) %copy-start) | copy-done | bytes 524312
  1.0 1.7 %split_cells.1 = (f32[16,2,32,128]{3,2,1,0:T(8,128)S(1)}, f32[9,2,32,128]{3,2,1,0:T(8,128)S(1)}, f32[9,2,32,128]{3,2,1,0:T(8,128)S(1)}) custom-call(f32[16,32,256]{2,1,0:T(8,128)S(1)} %copy-done), custom_call_target="tpu_custom_call" | custom-call | tf_op jit(solution)/shard_map/split_cells/pallas_call | solution.py:491
  2.7 6.9 %collective-permute-start = (f32[9,2,32,128]{3,2,1,0:T(8,128)S(1)}, f32[9,2,32,128]{3,2,1,0:T(8,128)S(1)}, u32[]{:S(2)}, u32[]{:S(2)}) collective-permute-start(f32[9,2,32,128]{3,2,1,0:T(8,128)S(1)} %get-tuple-element.17), channel_id=1, source_target_pairs={{8,16},{16,8},{24,32},{32,24},{40,48},{48,40},{56,64},{64,56},{72,... | collective-permute-start | bytes 884744 | tf_op jit(solution)/shard_map/ppermute | solution.py:501
  9.7 0.0 collective-permute-start.1
  9.7 4.4 %collective-permute-done.zo_ref.refs_1_ = f32[9,2,32,128]{3,2,1,0:T(8,128)S(1)} collective-permute-done((f32[9,2,32,128]{3,2,1,0:T(8,128)S(1)}, f32[9,2,32,128]{3,2,1,0:T(8,128)S(1)}, u32[]{:S(2)}, u32[]{:S(2)}) %collective-permute-start) | collective-permute-done | bytes 294944 | tf_op jit(solution)/shard_map/ppermute | solution.py:501
  14.1 0.0 collective-permute-done.1.ze_ref.refs_2_
  14.1 0.5 pack_rows.2
  14.5 5.8 %collective-permute-start.2 = (f32[2,312,128]{2,1,0:T(8,128)S(1)}, f32[2,312,128]{2,1,0:T(8,128)S(1)}, u32[]{:S(2)}, u32[]{:S(2)}) collective-permute-start(f32[2,312,128]{2,1,0:T(8,128)S(1)} %get-tuple-element.19), channel_id=1, source_target_pairs={{1,2},{2,1},{3,4},{4,3},{5,6},{6,5},{9,10},{10,9},{11,12},{12,11},... | collective-permute-start | bytes 958472 | tf_op jit(solution)/shard_map/ppermute | solution.py:504
  20.3 0.1 collective-permute-start.3
  20.4 5.1 %collective-permute-done.2.refs_3_ = f32[2,312,128]{2,1,0:T(8,128)S(1)} collective-permute-done((f32[2,312,128]{2,1,0:T(8,128)S(1)}, f32[2,312,128]{2,1,0:T(8,128)S(1)}, u32[]{:S(2)}, u32[]{:S(2)}) %collective-permute-start.2) | collective-permute-done | bytes 319520 | tf_op jit(solution)/shard_map/ppermute | solution.py:504
  25.5 1.9 %collective-permute-done.3.refs_4_ = f32[2,312,128]{2,1,0:T(8,128)S(1)} collective-permute-done((f32[2,312,128]{2,1,0:T(8,128)S(1)}, f32[2,312,128]{2,1,0:T(8,128)S(1)}, u32[]{:S(2)}, u32[]{:S(2)}) %collective-permute-start.3) | collective-permute-done | bytes 319520 | tf_op jit(solution)/shard_map/ppermute | solution.py:505
  27.4 22.1 %first_step.1 = (f32[16,2,32,128]{3,2,1,0:T(8,128)S(1)}, f32[9,2,32,128]{3,2,1,0:T(8,128)S(1)}, f32[9,2,32,128]{3,2,1,0:T(8,128)S(1)}, f32[2,2176,128]{2,1,0:T(8,128)S(1)}) custom-call(f32[16,2,32,128]{3,2,1,0:T(8,128)S(1)} %get-tuple-element.16.own_ref.refs_0_, f32[9,2,32,128]{3,2,1,0:T(8,128)S(1)} %collective-permute-done.zo_ref.refs_1_, ...), custom_call_target="tpu_custom_call" | custom-call | tf_op jit(solution)/shard_map/first_step/pallas_call | solution.py:511
  49.5 4.6 %collective-permute-start.4 = (f32[9,2,32,128]{3,2,1,0:T(8,128)S(1)}, f32[9,2,32,128]{3,2,1,0:T(8,128)S(1)}, u32[]{:S(2)}, u32[]{:S(2)}) collective-permute-start(f32[9,2,32,128]{3,2,1,0:T(8,128)S(1)} %get-tuple-element.22), channel_id=1, source_target_pairs={{8,16},{16,8},{24,32},{32,24},{40,48},{48,40},{56,64},{64,56},{72,... | collective-permute-start | bytes 884744 | tf_op jit(solution)/shard_map/ppermute | solution.py:501
  54.2 0.0 collective-permute-start.5
  54.2 5.2 %collective-permute-done.4.zo_ref.refs_1_ = f32[9,2,32,128]{3,2,1,0:T(8,128)S(1)} collective-permute-done((f32[9,2,32,128]{3,2,1,0:T(8,128)S(1)}, f32[9,2,32,128]{3,2,1,0:T(8,128)S(1)}, u32[]{:S(2)}, u32[]{:S(2)}) %collective-permute-start.4) | collective-permute-done | bytes 294944 | tf_op jit(solution)/shard_map/ppermute | solution.py:501
  59.4 0.0 collective-permute-done.5.ze_ref.refs_2_
  59.4 0.5 pack_rows.3
  59.9 3.9 %collective-permute-start.6 = (f32[2,312,128]{2,1,0:T(8,128)S(1)}, f32[2,312,128]{2,1,0:T(8,128)S(1)}, u32[]{:S(2)}, u32[]{:S(2)}) collective-permute-start(f32[2,312,128]{2,1,0:T(8,128)S(1)} %get-tuple-element.24), channel_id=1, source_target_pairs={{1,2},{2,1},{3,4},{4,3},{5,6},{6,5},{9,10},{10,9},{11,12},{12,11},... | collective-permute-start | bytes 958472 | tf_op jit(solution)/shard_map/ppermute | solution.py:504
  63.8 0.1 collective-permute-start.7
  63.9 7.0 %collective-permute-done.6.refs_3_ = f32[2,312,128]{2,1,0:T(8,128)S(1)} collective-permute-done((f32[2,312,128]{2,1,0:T(8,128)S(1)}, f32[2,312,128]{2,1,0:T(8,128)S(1)}, u32[]{:S(2)}, u32[]{:S(2)}) %collective-permute-start.6) | collective-permute-done | bytes 319520 | tf_op jit(solution)/shard_map/ppermute | solution.py:504
  70.8 0.0 collective-permute-done.7.refs_4_
  70.8 23.7 %next_step.1 = f32[16,32,256]{2,1,0:T(8,128)} custom-call(f32[16,2,32,128]{3,2,1,0:T(8,128)S(1)} %get-tuple-element.21.own_ref.refs_0_, f32[9,2,32,128]{3,2,1,0:T(8,128)S(1)} %collective-permute-done.4.zo_ref.refs_1_, f32[9,2,32,128]{3,2,1,0:T(8,128)S(1)} %collective-permute-done.5.ze_ref.refs_2_, f32[2,312,128]{2,1,0:T(8,128)S(1)} %collective-permute-done.6.refs_3_, ...), custom_call_target="tpu_custom_call" | custom-call | tf_op jit(solution)/shard_map/next_step/pallas_call | solution.py:511
Async XLA Ops:
  0.0 1.0 %copy-start = (f32[16,32,256]{2,1,0:T(8,128)S(1)}, f32[16,32,256]{2,1,0:T(8,128)}, u32[]{:S(2)}) copy-start(f32[16,32,256]{2,1,0:T(8,128)} %own_ref.1) | copy-start | bytes 1572868
  2.7 11.4 %collective-permute-start = (f32[9,2,32,128]{3,2,1,0:T(8,128)S(1)}, f32[9,2,32,128]{3,2,1,0:T(8,128)S(1)}, u32[]{:S(2)}, u32[]{:S(2)}) collective-permute-start(f32[9,2,32,128]{3,2,1,0:T(8,128)S(1)} %get-tuple-element.17), channel_id=1, source_target_pairs={{8,16},{16,8},{24,32},{32,24},{40,48},{48,40},{56,64},{64,56},{72,... | collective-permute-start | bytes 884744 | tf_op jit(solution)/shard_map/ppermute | solution.py:501
  9.7 4.4 %collective-permute-start.1 = (f32[9,2,32,128]{3,2,1,0:T(8,128)S(1)}, f32[9,2,32,128]{3,2,1,0:T(8,128)S(1)}, u32[]{:S(2)}, u32[]{:S(2)}) collective-permute-start(f32[9,2,32,128]{3,2,1,0:T(8,128)S(1)} %get-tuple-element.18), channel_id=1, source_target_pairs={{0,8},{8,0},{16,24},{24,16},{32,40},{40,32},{48,56},{56,48},{64,72... | collective-permute-start | bytes 884744 | tf_op jit(solution)/shard_map/ppermute | solution.py:502
  14.5 11.0 %collective-permute-start.2 = (f32[2,312,128]{2,1,0:T(8,128)S(1)}, f32[2,312,128]{2,1,0:T(8,128)S(1)}, u32[]{:S(2)}, u32[]{:S(2)}) collective-permute-start(f32[2,312,128]{2,1,0:T(8,128)S(1)} %get-tuple-element.19), channel_id=1, source_target_pairs={{1,2},{2,1},{3,4},{4,3},{5,6},{6,5},{9,10},{10,9},{11,12},{12,11},... | collective-permute-start | bytes 958472 | tf_op jit(solution)/shard_map/ppermute | solution.py:504
  20.3 7.1 %collective-permute-start.3 = (f32[2,312,128]{2,1,0:T(8,128)S(1)}, f32[2,312,128]{2,1,0:T(8,128)S(1)}, u32[]{:S(2)}, u32[]{:S(2)}) collective-permute-start(f32[2,312,128]{2,1,0:T(8,128)S(1)} %get-tuple-element.20), channel_id=1, source_target_pairs={{0,1},{1,0},{2,3},{3,2},{4,5},{5,4},{6,7},{7,6},{8,9},{9,8},{10,11... | collective-permute-start | bytes 958472 | tf_op jit(solution)/shard_map/ppermute | solution.py:505
  49.5 9.8 %collective-permute-start.4 = (f32[9,2,32,128]{3,2,1,0:T(8,128)S(1)}, f32[9,2,32,128]{3,2,1,0:T(8,128)S(1)}, u32[]{:S(2)}, u32[]{:S(2)}) collective-permute-start(f32[9,2,32,128]{3,2,1,0:T(8,128)S(1)} %get-tuple-element.22), channel_id=1, source_target_pairs={{8,16},{16,8},{24,32},{32,24},{40,48},{48,40},{56,64},{64,56},{72,... | collective-permute-start | bytes 884744 | tf_op jit(solution)/shard_map/ppermute | solution.py:501
  54.2 5.2 %collective-permute-start.5 = (f32[9,2,32,128]{3,2,1,0:T(8,128)S(1)}, f32[9,2,32,128]{3,2,1,0:T(8,128)S(1)}, u32[]{:S(2)}, u32[]{:S(2)}) collective-permute-start(f32[9,2,32,128]{3,2,1,0:T(8,128)S(1)} %get-tuple-element.23), channel_id=1, source_target_pairs={{0,8},{8,0},{16,24},{24,16},{32,40},{40,32},{48,56},{56,48},{64,72... | collective-permute-start | bytes 884744 | tf_op jit(solution)/shard_map/ppermute | solution.py:502
  59.9 11.0 %collective-permute-start.6 = (f32[2,312,128]{2,1,0:T(8,128)S(1)}, f32[2,312,128]{2,1,0:T(8,128)S(1)}, u32[]{:S(2)}, u32[]{:S(2)}) collective-permute-start(f32[2,312,128]{2,1,0:T(8,128)S(1)} %get-tuple-element.24), channel_id=1, source_target_pairs={{1,2},{2,1},{3,4},{4,3},{5,6},{6,5},{9,10},{10,9},{11,12},{12,11},... | collective-permute-start | bytes 958472 | tf_op jit(solution)/shard_map/ppermute | solution.py:504
  63.8 7.1 %collective-permute-start.7 = (f32[2,312,128]{2,1,0:T(8,128)S(1)}, f32[2,312,128]{2,1,0:T(8,128)S(1)}, u32[]{:S(2)}, u32[]{:S(2)}) collective-permute-start(f32[2,312,128]{2,1,0:T(8,128)S(1)} %get-tuple-element.25), channel_id=1, source_target_pairs={{0,1},{1,0},{2,3},{3,2},{4,5},{5,4},{6,7},{7,6},{8,9},{9,8},{10,11... | collective-permute-start | bytes 958472 | tf_op jit(solution)/shard_map/ppermute | solution.py:505

commit v2 on v1

v2 whole, which is shorter than its diff:
```python
import functools

import jax
import jax.numpy as jnp
from jax import lax
from jax.experimental import pallas as pl
from jax.experimental.pallas import tpu as pltpu
from jax.sharding import PartitionSpec as P

STEPS = 2
TAU = 0.3
EPS = 0.75e-6

DEEP = 9
PITCH = 64
ROW0 = 16
f32 = jnp.float32


def triple(g, h, curve):
    lean = 1.5 * curve
    mid = curve * curve + (0.75 * (g * h) + EPS)
    left = mid + lean * h
    right = mid - lean * g
    return left * left, mid * mid, right * right


def face(a, b, c, jump_low, jump_high, base_back, base_fore):
    p = b * c
    q = a * c
    r = a * b
    half = 0.5 * (p + r) + 3.0 * q
    pj = p * jump_low
    rj = r * jump_high
    back = base_back - (pj + 1.5 * rj) / (half + r)
    fore = base_fore - (1.5 * pj + rj) / (half + p)
    return back, fore


def upwind(back, fore, side):
    best = jnp.maximum(jnp.maximum(side * back, side * fore), 0.0)
    return best * best


def bases(center, low_slope, high_slope):
    six = 6.0 * center
    both = low_slope + high_slope
    return six + (both + high_slope), (both + low_slope) - six


def at(z, r, n=8):
    return pl.ds(z * PITCH + r, n)


def z_pass(src, side, acc, margin, r0, tiles, first_tile=0, tile_step=1):
    first = DEEP - margin
    last = DEEP + 16 + margin

    def column(i, carry):
        t = first_tile + tile_step * i
        r = r0 + 8 * t
        state = [dict(), dict()]
        for k in range(first - 1, last):
            for h in range(2):
                s = state[h]

                def u(z):
                    if ("u", z) not in s:
                        s["u", z] = src[h, at(z, r), :]
                    return s["u", z]

                def d(z):
                    if ("d", z) not in s:
                        s["d", z] = u(z + 1) - u(z)
                    return s["d", z]

                def e(z):
                    if ("e", z) not in s:
                        s["e", z] = d(z + 1) - d(z)
                    return s["e", z]

                def c(z):
                    if ("c", z) not in s:
                        s["c", z] = e(z) - e(z - 1)
                    return s["c", z]

                def j(z):
                    if ("j", z) not in s:
                        s["j", z] = c(z) - c(z - 1)
                    return s["j", z]

                def tr(z):
                    if ("t", z) not in s:
                        s["t", z] = triple(e(z - 1), e(z), c(z))
                    return s["t", z]

                base_back, base_fore = bases(d(k), e(k - 1), e(k))
                back, fore = face(
                    tr(k - 1)[0], tr(k)[1], tr(k + 1)[2], j(k), j(k + 1), base_back, base_fore
                )
                if k >= first:
                    acc[h, pl.ds((k - first) * 48 + 8 * t, 8), :] += upwind(
                        s["back"], fore, side[h, at(k, r), :]
                    )
                s["back"] = back
        return carry

    lax.fori_loop(0, tiles, column, 0)


def y_pass(src, side, rate_of, acc, scr, put, combine, margin, r0, tiles, face_tiles, triple_rows):
    first = DEEP - margin
    count = 16 + 2 * margin
    left_s, mid_s, right_s, curve_s, diff_s, fore_s = scr

    def two_planes(i, carry):
        for sub in range(2):
            zi = i * 2 + sub
            z = first + zi
            for h in range(2):
                slot = sub * 2 + h
                for row in triple_rows:
                    r = r0 - 2 + row
                    u0 = src[h, at(z, r - 1), :]
                    u1 = src[h, at(z, r), :]
                    u2 = src[h, at(z, r + 1), :]
                    u3 = src[h, at(z, r + 2), :]
                    d1 = u2 - u1
                    g = d1 - (u1 - u0)
                    e = (u3 - u2) - d1
                    curve = e - g
                    rows = pl.ds(row, 8)
                    left_s[slot, rows, :], mid_s[slot, rows, :], right_s[slot, rows, :] = triple(g, e, curve)
                    curve_s[slot, rows, :] = curve
                    diff_s[slot, rows, :] = d1
            for h in range(2):
                slot = sub * 2 + h
                backs = []
                for t in range(face_tiles):
                    lo, me, hi = pl.ds(8 * t, 8), pl.ds(8 * t + 1, 8), pl.ds(8 * t + 2, 8)
                    dl, dm, dh = diff_s[slot, lo, :], diff_s[slot, me, :], diff_s[slot, hi, :]
                    cm = curve_s[slot, me, :]
                    five = 5.0 * dm
                    back, fore = face(
                        left_s[slot, lo, :],
                        mid_s[slot, me, :],
                        right_s[slot, hi, :],
                        cm - curve_s[slot, lo, :],
                        curve_s[slot, hi, :] - cm,
                        five + ((dh + dh) - dl),
                        (dh - (dl + dl)) - five,
                    )
                    fore_s[slot, pl.ds(8 * t, 8), :] = fore
                    backs.append(back)
                for t in range(tiles):
                    r = r0 + 8 * t
                    fore = fore_s[slot, pl.ds(8 * t + 1, 8), :]
                    total = acc[h, pl.ds(zi * 48 + 8 * t, 8), :] + upwind(
                        backs[t], fore, side[h, at(z, r), :]
                    )
                    norm = total * lax.rsqrt(jnp.maximum(total, 1e-30))
                    stepped = src[h, at(z, r), :] + rate_of[h, at(z, r), :] * ((1.0 / 6.0) * norm - 1.0)
                    put(h, zi, t, r, combine(h, z, r, stepped))
        return carry

    lax.fori_loop(0, count // 2, two_planes, 0)


def x_pass(load, side, acc, scr, z0, count, acc0, r0, tile_list, unroll):
    lane = lax.broadcasted_iota(jnp.int32, (8, 128), 1)
    below_last = lane < 127
    below_two = lane < 126
    above_first = lane > 0
    shifted, finished = scr

    def shift(z, s):
        for t in tile_list:
            even, odd = load(0, z, r0 + 8 * t), load(1, z, r0 + 8 * t)
            rows = pl.ds(8 * t, 8)
            shifted[s, 0, rows, :] = jnp.where(above_first, pltpu.roll(even, 1, 1), even)
            shifted[s, 1, rows, :] = jnp.where(above_first, pltpu.roll(odd, 1, 1), even)
            shifted[s, 2, rows, :] = jnp.where(below_last, pltpu.roll(even, 127, 1), odd)
            odd_up = jnp.where(below_last, pltpu.roll(odd, 127, 1), odd)
            shifted[s, 3, rows, :] = odd_up
            shifted[s, 4, rows, :] = jnp.where(below_two, pltpu.roll(even, 126, 1), odd_up)

    def put(h, k, t, back, fore):
        wind = side[h, at(z0 + k, r0 + 8 * t), :]
        acc[h, pl.ds((acc0 + k) * 48 + 8 * t, 8), :] = upwind(back, fore, wind)

    def finish_even(k, s):
        for t in tile_list:
            rows = pl.ds(8 * t, 8)
            put(0, k, t, finished[s, 0, rows, :], finished[s, 1, rows, :])

    def faces(k, s):
        z = z0 + k
        for t in tile_list:
            rows = pl.ds(8 * t, 8)
            u = [
                shifted[s, 0, rows, :],
                shifted[s, 1, rows, :],
                load(0, z, r0 + 8 * t),
                load(1, z, r0 + 8 * t),
                shifted[s, 2, rows, :],
                shifted[s, 3, rows, :],
                shifted[s, 4, rows, :],
            ]
            d = [u[i + 1] - u[i] for i in range(6)]
            e = [d[i + 1] - d[i] for i in range(5)]
            c = [e[i + 1] - e[i] for i in range(4)]
            jump = [c[i + 1] - c[i] for i in range(3)]
            tri = [triple(e[i], e[i + 1], c[i]) for i in range(4)]
            back_even, fore_even = face(
                tri[0][0], tri[1][1], tri[2][2], jump[0], jump[1], *bases(d[2], e[1], e[2])
            )
            back_odd, fore_odd = face(
                tri[1][0], tri[2][1], tri[3][2], jump[1], jump[2], *bases(d[3], e[2], e[3])
            )
            p = tri[0][1] * tri[1][2]
            r = (1.5 * EPS * EPS) * tri[0][1]
            edge = (e[1] + e[1]) - (p * c[0] + r * jump[0]) / (
                (0.5 * p + r) + (3.0 * EPS * EPS) * tri[1][2]
            )
            finished[s, 0, rows, :] = jnp.where(above_first, pltpu.roll(back_odd, 1, 1), edge)
            finished[s, 1, rows, :] = fore_even
            put(1, k, t, back_even, fore_odd)

    shift(z0, 0)

    def planes(i, carry):
        for s in range(unroll):
            k = unroll * i + s
            shift(z0 + k + 1, (s + 1) % unroll)
            finish_even(jnp.maximum(k - 1, 0) if s == 0 else k - 1, (s - 1) % unroll)
            faces(k, s)
        return carry

    lax.fori_loop(0, count // unroll, planes, 0)
    finish_even(count - 1, unroll - 1)


def from_work(work):
    return lambda h, z, r: work[h, at(z, r), :]


def position():
    gz, gy = lax.axis_index("gz"), lax.axis_index("gy")
    return lax.rem(gz, 2), lax.rem(gy, 2), gy == 0, gy == lax.axis_size("gy") - 1


def load_planes(work, ref, start, count):
    def one(k, carry):
        for t in range(4):
            for h in range(2):
                work[h, at(start + k, ROW0 + 8 * t), :] = ref[k, h, 8 * t : 8 * t + 8, :]
        return carry

    lax.fori_loop(0, count, one, 0)


def load_rows(work, yo_ref, ye_ref, odd_y):
    def both(low, high):
        def one(z, carry):
            for h in range(2):
                work[h, at(z, ROW0 - 8), :] = low[h, pl.ds(8 * z, 8), :]
                work[h, at(z, ROW0 - 9, 1), :] = low[h, pl.ds(272 + z, 1), :]
                work[h, at(z, ROW0 + 32), :] = high[h, pl.ds(8 * z, 8), :]
                work[h, at(z, ROW0 + 40, 1), :] = high[h, pl.ds(272 + z, 1), :]
            return carry

        lax.fori_loop(0, 34, one, 0)

    @pl.when(odd_y == 0)
    def _():
        both(yo_ref, ye_ref)

    @pl.when(odd_y == 1)
    def _():
        both(ye_ref, yo_ref)


def signs(load, weight, side, z0, count, row_list):
    def one(k, carry):
        z = z0 + k
        for h in range(2):
            for r in row_list:
                v = load(h, z, r)
                weight[h, at(z, r), :] = (-TAU) * (v * lax.rsqrt(v * v + 1.0))
                side[h, at(z, r), :] = jnp.where(v >= 0.0, 1.0, -1.0)
        return carry

    lax.fori_loop(0, count, one, 0)


def edge_rows(work, start, count, far, is_first, is_last):
    @pl.when(is_first)
    def _():
        def one(k, carry):
            z = start + k
            for h in range(2):
                row = work[h, at(z, ROW0, 1), :]
                work[h, at(z, ROW0 - 8), :] = jnp.broadcast_to(row, (8, 128))
                if far:
                    work[h, at(z, ROW0 - 9, 1), :] = row
            return carry

        lax.fori_loop(0, count, one, 0)

    @pl.when(is_last)
    def _():
        def one(k, carry):
            z = start + k
            for h in range(2):
                row = work[h, at(z, ROW0 + 31, 1), :]
                work[h, at(z, ROW0 + 32), :] = jnp.broadcast_to(row, (8, 128))
                if far:
                    work[h, at(z, ROW0 + 40, 1), :] = row
            return carry

        lax.fori_loop(0, count, one, 0)


OWN_ROWS = tuple(ROW0 + 8 * t for t in range(4))
WIDE = ROW0 - 8
OWN_TILES = (1, 2, 3, 4)


def own_kernel(initial, own_ref, *refs):
    if initial:
        weight, side, acc, shifted, finished = refs

        def load(h, z, r):
            return own_ref[z - DEEP, h, pl.ds(r - ROW0, 8), :]

        signs(load, weight, side, DEEP, 16, OWN_ROWS)
    else:
        side, acc, shifted, finished = refs

    def load_clamped(h, z, r):
        return own_ref[jnp.minimum(z - DEEP, 15), h, pl.ds(r - ROW0, 8), :]

    x_pass(load_clamped, side, acc, (shifted, finished), DEEP, 16, 6, WIDE, OWN_TILES, 2)


def planes_kernel(initial, own_ref, zo_ref, ze_ref, *refs):
    if initial:
        _, _, _, weight, side, acc, u, shifted, finished = refs
    else:
        side, _, acc, u, shifted, finished = refs
    odd_z, _, _, _ = position()
    load_planes(u, own_ref, DEEP, 16)
    load_planes(u, zo_ref, 25 * odd_z, DEEP)
    load_planes(u, ze_ref, 25 * (1 - odd_z), DEEP)
    load = from_work(u)
    for z0 in (3, 25):
        if initial:
            signs(load, weight, side, z0, 6, OWN_ROWS)
        x_pass(load, side, acc, (shifted, finished), z0, 6, z0 - 3, WIDE, OWN_TILES, 2)
    z_pass(u, side, acc, 6, WIDE, 4, 1)


def rest_kernel(initial, yo_ref, ye_ref, *refs):
    refs = list(refs)
    if initial:
        out_ref, so_ref, se_ref, weight, side, acc, u = refs[4:11]
        refs = refs[11:]
    else:
        weight, side = refs[:2]
        out_ref, acc, u = refs[4:7]
        refs = refs[7:]
    first, second = refs[:2]
    scr = refs[2:8]
    x_scr = refs[8:10]
    third = refs[10]
    odd_z, odd_y, is_first, is_last = position()
    load_rows(u, yo_ref, ye_ref, odd_y)
    edge_rows(u, 0, 34, True, is_first, is_last)
    if initial:
        signs(from_work(u), weight, side, 3, 28, (WIDE, WIDE + 40))

    def store(work, start):
        def put(h, zi, t, r, value):
            work[h, at(start + zi, r), :] = value

        return put

    def put_out(h, zi, t, r, value):
        out_ref[zi, h, 8 * t : 8 * t + 8, :] = value

    def put_third(h, zi, t, r, value):
        third[h, pl.ds(zi * 32 + 8 * t, 8), :] = value

    def second_stage(h, z, r, v):
        return 0.75 * u[h, at(z, r), :] + 0.25 * v

    def third_stage(h, z, r, v):
        return (1.0 / 3.0) * u[h, at(z, r), :] + (2.0 / 3.0) * v

    x_pass(from_work(u), side, acc, x_scr, 3, 28, 0, WIDE, (0, 5), 4)
    z_pass(u, side, acc, 6, WIDE, 2, 0, 5)
    y_pass(
        u, side, weight, acc, scr, store(first, 3), lambda h, z, r, v: v, 6, WIDE, 6, 6, (1, 9, 17, 25, 33, 41)
    )
    edge_rows(first, 3, 28, False, is_first, is_last)
    x_pass(from_work(first), side, acc, x_scr, 6, 22, 0, ROW0 - 3, range(5), 2)
    z_pass(first, side, acc, 3, ROW0 - 3, 5)
    y_pass(
        first, side, weight, acc, scr, store(second, 6), second_stage, 3, ROW0 - 3, 5, 5, (0, 8, 16, 24, 32, 40)
    )
    edge_rows(second, 6, 22, False, is_first, is_last)
    x_pass(from_work(second), side, acc, x_scr, 9, 16, 0, ROW0, range(4), 2)
    z_pass(second, side, acc, 0, ROW0, 4)
    y_pass(
        second,
        side,
        weight,
        acc,
        scr,
        put_out if initial else put_third,
        third_stage,
        0,
        ROW0,
        4,
        5,
        (0, 8, 16, 24, 32),
    )

    if initial:

        def slabs(k, carry):
            so_ref[k] = out_ref[k + 7 * odd_z]
            se_ref[k] = out_ref[k + 7 * (1 - odd_z)]
            return carry

        lax.fori_loop(0, DEEP, slabs, 0)
    else:
        lane = lax.broadcasted_iota(jnp.int32, (8, 128), 1)
        even = (lane & 1) == 0
        half = lane >> 1

        def merge(k, carry):
            for t in range(4):
                rows = pl.ds(k * 32 + 8 * t, 8)
                for h in range(2):
                    parts = [jnp.take_along_axis(third[p, rows, :], half + 64 * h, axis=1) for p in range(2)]
                    out_ref[k, 8 * t : 8 * t + 8, 128 * h : 128 * h + 128] = jnp.where(even, *parts)
            return carry

        lax.fori_loop(0, 16, merge, 0)


def split_kernel(own_ref, out_ref, so_ref, se_ref):
    odd_z = lax.rem(lax.axis_index("gz"), 2)
    lane = lax.broadcasted_iota(jnp.int32, (8, 128), 1)
    low = lane < 64
    twice = (lane & 63) * 2

    def plane(k, carry):
        for t in range(4):
            v = [own_ref[k, 8 * t : 8 * t + 8, 128 * h : 128 * h + 128] for h in range(2)]
            for p in range(2):
                parts = [jnp.take_along_axis(x, twice + p, axis=1) for x in v]
                out_ref[k, p, 8 * t : 8 * t + 8, :] = jnp.where(low, *parts)
        return carry

    lax.fori_loop(0, 16, plane, 0)

    def slabs(k, carry):
        so_ref[k] = out_ref[k + 7 * odd_z]
        se_ref[k] = out_ref[k + 7 * (1 - odd_z)]
        return carry

    lax.fori_loop(0, DEEP, slabs, 0)


def pack_kernel(own_ref, zo_ref, ze_ref, yo_ref, ye_ref):
    odd_z = lax.rem(lax.axis_index("gz"), 2)
    odd_y = lax.rem(lax.axis_index("gy"), 2)

    def fill(out, main, extra):
        def planes(ref, start, count):
            def one(k, carry):
                for h in range(2):
                    out[h, pl.ds(8 * (start + k), 8), :] = ref[k, h, main : main + 8, :]
                    out[h, pl.ds(272 + start + k, 1), :] = ref[k, h, extra : extra + 1, :]
                return carry

            lax.fori_loop(0, count, one, 0)

        planes(own_ref, DEEP, 16)
        planes(zo_ref, 25 * odd_z, DEEP)
        planes(ze_ref, 25 * (1 - odd_z), DEEP)
        out[:, 306:312, :] = jnp.zeros((2, 6, 128), f32)

    @pl.when(odd_y == 0)
    def _():
        fill(yo_ref, 0, 8)
        fill(ye_ref, 24, 23)

    @pl.when(odd_y == 1)
    def _():
        fill(yo_ref, 24, 23)
        fill(ye_ref, 0, 8)


def swaps(count, start, periodic):
    pairs = []
    for low in range(start, count, 2):
        if low + 1 < count or periodic:
            high = (low + 1) % count
            pairs += [(low, high), (high, low)]
    return pairs


VMEM = pl.BlockSpec(memory_space=pltpu.VMEM)
WORK = (2, 34 * PITCH, 128)
ACC = (2, 28 * 48, 128)


def call(kernel, name, args, outs, scratch=(), aliases=None, cycles=1000):
    result = pl.pallas_call(
        kernel,
        out_shape=[jax.ShapeDtypeStruct(shape, f32) for shape in outs],
        in_specs=[VMEM] * len(args),
        out_specs=[VMEM] * len(outs),
        scratch_shapes=[pltpu.VMEM(shape, f32) for shape in scratch],
        input_output_aliases=aliases or {},
        compiler_params=pltpu.CompilerParams(vmem_limit_bytes=24 * 1024 * 1024),
        cost_estimate=pl.CostEstimate(flops=4096 * cycles, bytes_accessed=4096 * cycles, transcendentals=0),
        name=name,
    )(*args)
    return result


def per_device(level_set):
    n_z, n_y = lax.axis_size("gz"), lax.axis_size("gy")
    z_odd, z_even = swaps(n_z, 1, True), swaps(n_z, 0, True)
    y_odd, y_even = swaps(n_y, 1, False), swaps(n_y, 0, False)
    split, deep, slab = (16, 2, 32, 128), (DEEP, 2, 32, 128), (2, 312, 128)
    shifts = [(2, 5, 48, 128), (2, 2, 48, 128)]
    rest_scratch = [WORK] * 2 + [(4, 56, 128)] * 6 + [(4, 5, 48, 128), (4, 2, 48, 128), (2, 512, 128)]
    field, z_send_odd, z_send_even = call(split_kernel, "split_cells", (level_set,), [split, deep, deep])
    weight = side = None
    for step in range(STEPS):
        initial = step == 0
        zo = lax.ppermute(z_send_odd, "gz", z_odd)
        ze = lax.ppermute(z_send_even, "gz", z_even)
        own = functools.partial(own_kernel, initial)
        planes = functools.partial(planes_kernel, initial)
        rest = functools.partial(rest_kernel, initial)
        if initial:
            weight, side, acc = call(own, "own_planes", (field,), [WORK, WORK, ACC], shifts, cycles=4000)
        else:
            (acc,) = call(own, "own_planes_next", (field, side), [ACC], shifts, cycles=4000)
        y_send_odd, y_send_even = call(pack_kernel, "pack_rows", (field, zo, ze), [slab, slab])
        yo = lax.ppermute(y_send_odd, "gy", y_odd)
        ye = lax.ppermute(y_send_even, "gy", y_even)
        if initial:
            weight, side, acc, u = call(
                planes,
                "ghost_planes",
                (field, zo, ze, weight, side, acc),
                [WORK, WORK, ACC, WORK],
                shifts,
                {3: 0, 4: 1, 5: 2},
                8000,
            )
            field, z_send_odd, z_send_even, weight, side, _, _ = call(
                rest,
                "first_step",
                (yo, ye, weight, side, acc, u),
                [split, deep, deep, WORK, WORK, ACC, WORK],
                rest_scratch,
                {2: 3, 3: 4, 4: 5, 5: 6},
                30000,
            )
        else:
            acc, u = call(
                planes,
                "ghost_planes_next",
                (field, zo, ze, side, acc),
                [ACC, WORK],
                shifts,
                {4: 0},
                8000,
            )
            field, _, _ = call(
                rest,
                "next_step",
                (yo, ye, weight, side, acc, u),
                [(16, 32, 256), ACC, WORK],
                rest_scratch,
                {4: 1, 5: 2},
                30000,
            )
    return field


def solution(mesh):
    return jax.shard_map(
        per_device,
        mesh=mesh,
        in_specs=(P("gz", "gy", None),),
        out_specs=P("gz", "gy", None),
        check_vma=False,
    )
```

time: 94.7 us -> 86 us (0.908)
  waiting for transfers between devices: 23.6 us -> 13.3 us
  Pallas kernels: 48.4 us -> 49.9 us
    ppermute x2, waiting for transfers between devices: 12.1 us -> 2.05 us  [per_device(): yo = lax.ppermute(y_send_odd, 'gy', y_odd)]
    pallas_call x5 -> x9, Pallas kernels: 48.4 us -> 49.9 us  [call(): pl.pallas_call(kernel, out_shape=[jax.ShapeDtypeStruct(shape, f32) for sh...]
  transfers between devices with their start and end apart: 8 -> 8, of which waited for: 5 -> 4; matrix products, arithmetic and copies ran while one was open for 0% -> 0% of each run, Pallas kernels for 0% -> 12%
where the time goes in v2:
time: 86 us; the launch traced here: 85.8 us
  Pallas kernels  49.9 us (58%)
  starting transfers between devices  21.5 us (25%)
  waiting for transfers between devices  13.3 us (15%)
  local copies, waits for them, and re-layouts  1.04 us (1%)
    pallas_call x9, Pallas kernels, call(): pl.pallas_call(kernel, out_shape=[jax.ShapeDtypeStruct(shape, f32) for sh...  49.9 us
    ppermute x2, starting transfers between devices, per_device(): zo = lax.ppermute(z_send_odd, 'gz', z_odd)  11.6 us
    ppermute x2, starting transfers between devices, per_device(): yo = lax.ppermute(y_send_odd, 'gy', y_odd)  9.7 us
    ppermute x2, waiting for transfers between devices, per_device(): zo = lax.ppermute(z_send_odd, 'gz', z_odd)  9.62 us
    ppermute x2, waiting for transfers between devices, per_device(): yo = lax.ppermute(y_send_odd, 'gy', y_odd)  2.05 us
  transfers between devices with their start and end apart: 8, of which 4 were waited for; matrix products, arithmetic and copies ran while one was open for 0% of the time, Pallas kernels for 12%

profile of v2, /device:TPU:2, one launch (start us, length us, event | category | flops | bytes accessed | tf_op | source)
XLA Modules:
  0.0 85.8 jit_solution(15315450703901635913)
XLA Ops:
  0.0 1.0 %copy-done = f32[16,32,256]{2,1,0:T(8,128)S(1)} copy-done((f32[16,32,256]{2,1,0:T(8,128)S(1)}, f32[16,32,256]{2,1,0:T(8,128)}, u32[]{:S(2)}) %copy-start) | copy-done | bytes 524312
  1.0 1.7 %split_cells.1 = (f32[16,2,32,128]{3,2,1,0:T(8,128)S(1)}, f32[9,2,32,128]{3,2,1,0:T(8,128)S(1)}, f32[9,2,32,128]{3,2,1,0:T(8,128)S(1)}) custom-call(f32[16,32,256]{2,1,0:T(8,128)S(1)} %copy-done), custom_call_target="tpu_custom_call" | custom-call | flops 4096000 | bytes 4096000 | tf_op jit(solution)/shard_map/split_cells/pallas_call | solution.py:522
  2.7 6.9 %collective-permute-start = (f32[9,2,32,128]{3,2,1,0:T(8,128)S(1)}, f32[9,2,32,128]{3,2,1,0:T(8,128)S(1)}, u32[]{:S(2)}, u32[]{:S(2)}) collective-permute-start(f32[9,2,32,128]{3,2,1,0:T(8,128)S(1)} %get-tuple-element.28), channel_id=1, source_target_pairs={{8,16},{16,8},{24,32},{32,24},{40,48},{48,40},{56,64},{64,56},{72,... | collective-permute-start | bytes 884744 | tf_op jit(solution)/shard_map/ppermute | solution.py:547
  9.7 0.0 collective-permute-start.1
  9.7 4.4 %collective-permute-done.zo_ref = f32[9,2,32,128]{3,2,1,0:T(8,128)S(1)} collective-permute-done((f32[9,2,32,128]{3,2,1,0:T(8,128)S(1)}, f32[9,2,32,128]{3,2,1,0:T(8,128)S(1)}, u32[]{:S(2)}, u32[]{:S(2)}) %collective-permute-start) | collective-permute-done | bytes 294944 | tf_op jit(solution)/shard_map/ppermute | solution.py:547
  14.1 0.0 collective-permute-done.1.ze_ref
  14.1 0.5 pack_rows.2
  14.5 5.8 %collective-permute-start.2 = (f32[2,312,128]{2,1,0:T(8,128)S(1)}, f32[2,312,128]{2,1,0:T(8,128)S(1)}, u32[]{:S(2)}, u32[]{:S(2)}) collective-permute-start(f32[2,312,128]{2,1,0:T(8,128)S(1)} %get-tuple-element.30), channel_id=1, source_target_pairs={{1,2},{2,1},{3,4},{4,3},{5,6},{6,5},{9,10},{10,9},{11,12},{12,11},... | collective-permute-start | bytes 958472 | tf_op jit(solution)/shard_map/ppermute | solution.py:557
  20.3 0.1 collective-permute-start.3
  20.4 1.9 %own_planes.1 = (f32[2,2176,128]{2,1,0:T(8,128)S(1)}, f32[2,2176,128]{2,1,0:T(8,128)S(1)}, f32[2,1344,128]{2,1,0:T(8,128)S(1)}) custom-call(f32[16,2,32,128]{3,2,1,0:T(8,128)S(1)} %get-tuple-element.27.own_ref), custom_call_target="tpu_custom_call" | custom-call | flops 16384000 | bytes 16384000 | tf_op jit(solution)/shard_map/own_planes/pallas_call | solution.py:522
  22.4 3.4 %ghost_planes.1 = (f32[2,2176,128]{2,1,0:T(8,128)S(1)}, f32[2,2176,128]{2,1,0:T(8,128)S(1)}, f32[2,1344,128]{2,1,0:T(8,128)S(1)}, f32[2,2176,128]{2,1,0:T(8,128)S(1)}) custom-call(f32[16,2,32,128]{3,2,1,0:T(8,128)S(1)} %get-tuple-element.27.own_ref, ...), custom_call_target="tpu_custom_call", output_to_operand_aliasing={{0}: (3, {}), {1}: (4, {}), {2}: (5, {})} | custom-call | flops 32768000 | bytes 32768000 | tf_op jit(solution)/shard_map/ghost_planes/pallas_call | solution.py:522
  25.8 0.0 collective-permute-done.2.yo_ref
  25.8 1.6 %collective-permute-done.3.ye_ref = f32[2,312,128]{2,1,0:T(8,128)S(1)} collective-permute-done((f32[2,312,128]{2,1,0:T(8,128)S(1)}, f32[2,312,128]{2,1,0:T(8,128)S(1)}, u32[]{:S(2)}, u32[]{:S(2)}) %collective-permute-start.3) | collective-permute-done | bytes 319520 | tf_op jit(solution)/shard_map/ppermute | solution.py:558
  27.4 17.5 %first_step.1 = (f32[16,2,32,128]{3,2,1,0:T(8,128)S(1)}, f32[9,2,32,128]{3,2,1,0:T(8,128)S(1)}, f32[9,2,32,128]{3,2,1,0:T(8,128)S(1)}, f32[2,2176,128]{2,1,0:T(8...) custom-call(f32[2,312,128]{2,1,0:T(8,128)S(1)} %collective-permute-d, ...), custom_call_target="tpu_custom_call", output_to_operand_aliasing={{3}: (2, {}), {4}: (3, {}), {5}: (4, {}), {6}: (5, {})} | custom-call | flops 122880000 | bytes 122880000 | tf_op jit(solution)/shard_map/first_step/pallas_call | solution.py:522
  45.0 4.6 %collective-permute-start.4 = (f32[9,2,32,128]{3,2,1,0:T(8,128)S(1)}, f32[9,2,32,128]{3,2,1,0:T(8,128)S(1)}, u32[]{:S(2)}, u32[]{:S(2)}) collective-permute-start(f32[9,2,32,128]{3,2,1,0:T(8,128)S(1)} %get-tuple-element.40), channel_id=1, source_target_pairs={{8,16},{16,8},{24,32},{32,24},{40,48},{48,40},{56,64},{64,56},{72,... | collective-permute-start | bytes 884744 | tf_op jit(solution)/shard_map/ppermute | solution.py:547
  49.6 5.2 %collective-permute-done.4.zo_ref = f32[9,2,32,128]{3,2,1,0:T(8,128)S(1)} collective-permute-done((f32[9,2,32,128]{3,2,1,0:T(8,128)S(1)}, f32[9,2,32,128]{3,2,1,0:T(8,128)S(1)}, u32[]{:S(2)}, u32[]{:S(2)}) %collective-permute-start.4) | collective-permute-done | bytes 294944 | tf_op jit(solution)/shard_map/ppermute | solution.py:547
  54.8 0.5 pack_rows.3
  55.3 3.9 %collective-permute-start.6 = (f32[2,312,128]{2,1,0:T(8,128)S(1)}, f32[2,312,128]{2,1,0:T(8,128)S(1)}, u32[]{:S(2)}, u32[]{:S(2)}) collective-permute-start(f32[2,312,128]{2,1,0:T(8,128)S(1)} %get-tuple-element.42), channel_id=1, source_target_pairs={{1,2},{2,1},{3,4},{4,3},{5,6},{6,5},{9,10},{10,9},{11,12},{12,11},... | collective-permute-start | bytes 958472 | tf_op jit(solution)/shard_map/ppermute | solution.py:557
  59.2 0.1 collective-permute-start.7
  59.3 1.7 %own_planes_next.1.refs_1_ = f32[2,1344,128]{2,1,0:T(8,128)S(1)} custom-call(f32[16,2,32,128]{3,2,1,0:T(8,128)S(1)} %get-tuple-element.39.own_ref, f32[2,2176,128]{2,1,0:T(8,128)S(1)} %get-tuple-element.45.refs_0_.refs_1_), custom_call_target="tpu_custom_call" | custom-call | flops 16384000 | bytes 16384000 | tf_op jit(solution)/shard_map/own_planes_next/pallas_call | solution.py:522
  61.0 3.2 %ghost_planes_next.1 = (f32[2,1344,128]{2,1,0:T(8,128)S(1)}, f32[2,2176,128]{2,1,0:T(8,128)S(1)}) custom-call(f32[16,2,32,128]{3,2,1,0:T(8,128)S(1)} %get-tuple-element.39.own_ref, f32[9,2,32,128]{3,2,1,0:T(8,128)S(1)} %collective-permute-done.4.zo_ref, f32[9,2,32,128]{3,2,1,0:T(8,128)S(1)} %collective-permute-done.5.ze_ref, ...), custom_call_target="tpu_custom_call", output_to_operand_aliasing={{0}: (4, {})} | custom-call | flops 32768000 | bytes 32768000 | tf_op jit(solution)/shard_map/ghost_planes_next/pallas_call | solution.py:522
  64.2 2.0 %collective-permute-done.6.yo_ref = f32[2,312,128]{2,1,0:T(8,128)S(1)} collective-permute-done((f32[2,312,128]{2,1,0:T(8,128)S(1)}, f32[2,312,128]{2,1,0:T(8,128)S(1)}, u32[]{:S(2)}, u32[]{:S(2)}) %collective-permute-start.6) | collective-permute-done | bytes 319520 | tf_op jit(solution)/shard_map/ppermute | solution.py:557
  66.3 0.0 collective-permute-done.7.ye_ref
  66.3 19.5 %next_step.1 = (f32[16,32,256]{2,1,0:T(8,128)}, f32[2,1344,128]{2,1,0:T(8,128)S(1)}, f32[2,2176,128]{2,1,0:T(8,128)S(1)}) custom-call(f32[2,312,128]{2,1,0:T(8,128)S(1)} %collective-permute-done.6.yo_ref, f32[2,312,128]{2,1,0:T(8,128)S(1)} %collective-permute-done.7.ye_ref, ...), custom_call_target="tpu_custom_call", output_to_operand_aliasing={{1}: (4, {}), {2}: (5, {})} | custom-call | flops 122880000 | bytes 122880000 | tf_op jit(solution)/shard_map/next_step/pallas_call | solution.py:522
  (3 shorter events, 0.0 us)
Async XLA Ops:
  0.0 1.0 %copy-start = (f32[16,32,256]{2,1,0:T(8,128)S(1)}, f32[16,32,256]{2,1,0:T(8,128)}, u32[]{:S(2)}) copy-start(f32[16,32,256]{2,1,0:T(8,128)} %own_ref.1) | copy-start | bytes 1572868
  2.7 11.4 %collective-permute-start = (f32[9,2,32,128]{3,2,1,0:T(8,128)S(1)}, f32[9,2,32,128]{3,2,1,0:T(8,128)S(1)}, u32[]{:S(2)}, u32[]{:S(2)}) collective-permute-start(f32[9,2,32,128]{3,2,1,0:T(8,128)S(1)} %get-tuple-element.28), channel_id=1, source_target_pairs={{8,16},{16,8},{24,32},{32,24},{40,48},{48,40},{56,64},{64,56},{72,... | collective-permute-start | bytes 884744 | tf_op jit(solution)/shard_map/ppermute | solution.py:547
  9.7 4.4 %collective-permute-start.1 = (f32[9,2,32,128]{3,2,1,0:T(8,128)S(1)}, f32[9,2,32,128]{3,2,1,0:T(8,128)S(1)}, u32[]{:S(2)}, u32[]{:S(2)}) collective-permute-start(f32[9,2,32,128]{3,2,1,0:T(8,128)S(1)} %get-tuple-element.29), channel_id=1, source_target_pairs={{0,8},{8,0},{16,24},{24,16},{32,40},{40,32},{48,56},{56,48},{64,72... | collective-permute-start | bytes 884744 | tf_op jit(solution)/shard_map/ppermute | solution.py:548
  14.5 11.3 %collective-permute-start.2 = (f32[2,312,128]{2,1,0:T(8,128)S(1)}, f32[2,312,128]{2,1,0:T(8,128)S(1)}, u32[]{:S(2)}, u32[]{:S(2)}) collective-permute-start(f32[2,312,128]{2,1,0:T(8,128)S(1)} %get-tuple-element.30), channel_id=1, source_target_pairs={{1,2},{2,1},{3,4},{4,3},{5,6},{6,5},{9,10},{10,9},{11,12},{12,11},... | collective-permute-start | bytes 958472 | tf_op jit(solution)/shard_map/ppermute | solution.py:557
  20.3 7.1 %collective-permute-start.3 = (f32[2,312,128]{2,1,0:T(8,128)S(1)}, f32[2,312,128]{2,1,0:T(8,128)S(1)}, u32[]{:S(2)}, u32[]{:S(2)}) collective-permute-start(f32[2,312,128]{2,1,0:T(8,128)S(1)} %get-tuple-element.31), channel_id=1, source_target_pairs={{0,1},{1,0},{2,3},{3,2},{4,5},{5,4},{6,7},{7,6},{8,9},{9,8},{10,11... | collective-permute-start | bytes 958472 | tf_op jit(solution)/shard_map/ppermute | solution.py:558
  45.0 9.8 %collective-permute-start.4 = (f32[9,2,32,128]{3,2,1,0:T(8,128)S(1)}, f32[9,2,32,128]{3,2,1,0:T(8,128)S(1)}, u32[]{:S(2)}, u32[]{:S(2)}) collective-permute-start(f32[9,2,32,128]{3,2,1,0:T(8,128)S(1)} %get-tuple-element.40), channel_id=1, source_target_pairs={{8,16},{16,8},{24,32},{32,24},{40,48},{48,40},{56,64},{64,56},{72,... | collective-permute-start | bytes 884744 | tf_op jit(solution)/shard_map/ppermute | solution.py:547
  49.6 5.2 %collective-permute-start.5 = (f32[9,2,32,128]{3,2,1,0:T(8,128)S(1)}, f32[9,2,32,128]{3,2,1,0:T(8,128)S(1)}, u32[]{:S(2)}, u32[]{:S(2)}) collective-permute-start(f32[9,2,32,128]{3,2,1,0:T(8,128)S(1)} %get-tuple-element.41), channel_id=1, source_target_pairs={{0,8},{8,0},{16,24},{24,16},{32,40},{40,32},{48,56},{56,48},{64,72... | collective-permute-start | bytes 884744 | tf_op jit(solution)/shard_map/ppermute | solution.py:548
  55.3 11.0 %collective-permute-start.6 = (f32[2,312,128]{2,1,0:T(8,128)S(1)}, f32[2,312,128]{2,1,0:T(8,128)S(1)}, u32[]{:S(2)}, u32[]{:S(2)}) collective-permute-start(f32[2,312,128]{2,1,0:T(8,128)S(1)} %get-tuple-element.42), channel_id=1, source_target_pairs={{1,2},{2,1},{3,4},{4,3},{5,6},{6,5},{9,10},{10,9},{11,12},{12,11},... | collective-permute-start | bytes 958472 | tf_op jit(solution)/shard_map/ppermute | solution.py:557
  59.2 7.1 %collective-permute-start.7 = (f32[2,312,128]{2,1,0:T(8,128)S(1)}, f32[2,312,128]{2,1,0:T(8,128)S(1)}, u32[]{:S(2)}, u32[]{:S(2)}) collective-permute-start(f32[2,312,128]{2,1,0:T(8,128)S(1)} %get-tuple-element.43), channel_id=1, source_target_pairs={{0,1},{1,0},{2,3},{3,2},{4,5},{5,4},{6,7},{7,6},{8,9},{9,8},{10,11... | collective-permute-start | bytes 958472 | tf_op jit(solution)/shard_map/ppermute | solution.py:558

commit v3 on v2

--- a/solution.py
+++ b/solution.py
@@ -52,7 +52,7 @@
     return pl.ds(z * PITCH + r, n)
 
 
-def z_pass(src, side, acc, margin, r0, tiles, first_tile=0, tile_step=1):
+def z_pass(src, side, acc, margin, r0, tiles, first_tile=0, tile_step=1, acc0=0, fresh=False):
     first = DEEP - margin
     last = DEEP + 16 + margin
 
@@ -99,74 +99,75 @@
                     tr(k - 1)[0], tr(k)[1], tr(k + 1)[2], j(k), j(k + 1), base_back, base_fore
                 )
                 if k >= first:
-                    acc[h, pl.ds((k - first) * 48 + 8 * t, 8), :] += upwind(
-                        s["back"], fore, side[h, at(k, r), :]
-                    )
+                    rows = pl.ds((acc0 + k - first) * 48 + 8 * t, 8)
+                    share = upwind(s["back"], fore, side[h, at(k, r), :])
+                    acc[h, rows, :] = share if fresh else acc[h, rows, :] + share
                 s["back"] = back
         return carry
 
     lax.fori_loop(0, tiles, column, 0)
 
 
-def y_pass(src, side, rate_of, acc, scr, put, combine, margin, r0, tiles, face_tiles, triple_rows):
+def y_plane(src, side, rate_of, acc, scr, put, combine, margin, r0, tiles, face_tiles, rows):
     first = DEEP - margin
-    count = 16 + 2 * margin
-    left_s, mid_s, right_s, curve_s, diff_s, fore_s = scr
-
+    left_s, mid_s, right_s, curve_s, diff_s, slope_s, fore_s = scr
+    triple_rows, slope_rows, diff_rows = rows
+
+    def plane(zi, sub):
+        z = first + zi
+        for h in range(2):
+            slot = sub * 2 + h
+            for row in diff_rows:
+                r = r0 - 2 + row
+                diff_s[slot, pl.ds(row + 1, 8), :] = src[h, at(z, r + 1), :] - src[h, at(z, r), :]
+            for row in slope_rows:
+                above, below = diff_s[slot, pl.ds(row + 2, 8), :], diff_s[slot, pl.ds(row + 1, 8), :]
+                slope_s[slot, pl.ds(row + 1, 8), :] = above - below
+            for row in triple_rows:
+                g, e = slope_s[slot, pl.ds(row, 8), :], slope_s[slot, pl.ds(row + 1, 8), :]
+                curve = e - g
+                rows = pl.ds(row, 8)
+                left_s[slot, rows, :], mid_s[slot, rows, :], right_s[slot, rows, :] = triple(g, e, curve)
+                curve_s[slot, rows, :] = curve
+        for h in range(2):
+            slot = sub * 2 + h
+            backs = []
+            for t in range(face_tiles):
+                lo, me, hi = pl.ds(8 * t, 8), pl.ds(8 * t + 1, 8), pl.ds(8 * t + 2, 8)
+                cm = curve_s[slot, me, :]
+                back, fore = face(
+                    left_s[slot, lo, :],
+                    mid_s[slot, me, :],
+                    right_s[slot, hi, :],
+                    cm - curve_s[slot, lo, :],
+                    curve_s[slot, hi, :] - cm,
+                    *bases(diff_s[slot, hi, :], slope_s[slot, me, :], slope_s[slot, hi, :]),
+                )
+                fore_s[slot, pl.ds(8 * t, 8), :] = fore
+                backs.append(back)
+            for t in range(tiles):
+                r = r0 + 8 * t
+                fore = fore_s[slot, pl.ds(8 * t + 1, 8), :]
+                total = acc[h, pl.ds(zi * 48 + 8 * t, 8), :] + upwind(
+                    backs[t], fore, side[h, at(z, r), :]
+                )
+                norm = total * lax.rsqrt(jnp.maximum(total, 1e-30))
+                stepped = src[h, at(z, r), :] + rate_of[h, at(z, r), :] * ((1.0 / 6.0) * norm - 1.0)
+                put(h, zi, t, r, combine(h, z, r, stepped))
+
+    return plane
+
+
+def y_pass(count, plane):
     def two_planes(i, carry):
-        for sub in range(2):
-            zi = i * 2 + sub
-            z = first + zi
-            for h in range(2):
-                slot = sub * 2 + h
-                for row in triple_rows:
-                    r = r0 - 2 + row
-                    u0 = src[h, at(z, r - 1), :]
-                    u1 = src[h, at(z, r), :]
-                    u2 = src[h, at(z, r + 1), :]
-                    u3 = src[h, at(z, r + 2), :]
-                    d1 = u2 - u1
-                    g = d1 - (u1 - u0)
-                    e = (u3 - u2) - d1
-                    curve = e - g
-                    rows = pl.ds(row, 8)
-                    left_s[slot, rows, :], mid_s[slot, rows, :], right_s[slot, rows, :] = triple(g, e, curve)
-                    curve_s[slot, rows, :] = curve
-                    diff_s[slot, rows, :] = d1
-            for h in range(2):
-                slot = sub * 2 + h
-                backs = []
-                for t in range(face_tiles):
-                    lo, me, hi = pl.ds(8 * t, 8), pl.ds(8 * t + 1, 8), pl.ds(8 * t + 2, 8)
-                    dl, dm, dh = diff_s[slot, lo, :], diff_s[slot, me, :], diff_s[slot, hi, :]
-                    cm = curve_s[slot, me, :]
-                    five = 5.0 * dm
-                    back, fore = face(
-                        left_s[slot, lo, :],
-                        mid_s[slot, me, :],
-                        right_s[slot, hi, :],
-                        cm - curve_s[slot, lo, :],
-                        curve_s[slot, hi, :] - cm,
-                        five + ((dh + dh) - dl),
-                        (dh - (dl + dl)) - five,
-                    )
-                    fore_s[slot, pl.ds(8 * t, 8), :] = fore
-                    backs.append(back)
-                for t in range(tiles):
-                    r = r0 + 8 * t
-                    fore = fore_s[slot, pl.ds(8 * t + 1, 8), :]
-                    total = acc[h, pl.ds(zi * 48 + 8 * t, 8), :] + upwind(
-                        backs[t], fore, side[h, at(z, r), :]
-                    )
-                    norm = total * lax.rsqrt(jnp.maximum(total, 1e-30))
-                    stepped = src[h, at(z, r), :] + rate_of[h, at(z, r), :] * ((1.0 / 6.0) * norm - 1.0)
-                    put(h, zi, t, r, combine(h, z, r, stepped))
+        plane(2 * i, 0)
+        plane(2 * i + 1, 1)
         return carry
 
     lax.fori_loop(0, count // 2, two_planes, 0)
 
 
-def x_pass(load, side, acc, scr, z0, count, acc0, r0, tile_list, unroll):
+def x_parts(load, side, acc, scr, z0, acc0, r0, tile_list, fresh):
     lane = lax.broadcasted_iota(jnp.int32, (8, 128), 1)
     below_last = lane < 127
     below_two = lane < 126
@@ -186,7 +187,9 @@
 
     def put(h, k, t, back, fore):
         wind = side[h, at(z0 + k, r0 + 8 * t), :]
-        acc[h, pl.ds((acc0 + k) * 48 + 8 * t, 8), :] = upwind(back, fore, wind)
+        rows = pl.ds((acc0 + k) * 48 + 8 * t, 8)
+        share = upwind(back, fore, wind)
+        acc[h, rows, :] = share if fresh else acc[h, rows, :] + share
 
     def finish_even(k, s):
         for t in tile_list:
@@ -226,18 +229,47 @@
             finished[s, 1, rows, :] = fore_even
             put(1, k, t, back_even, fore_odd)
 
-    shift(z0, 0)
+    return lambda k, s: shift(z0 + k, s), finish_even, faces
+
+
+def x_pass(load, side, acc, scr, z0, count, acc0, r0, tile_list):
+    shift, finish_even, faces = x_parts(load, side, acc, scr, z0, acc0, r0, tile_list, True)
+    shift(0, 0)
 
     def planes(i, carry):
-        for s in range(unroll):
-            k = unroll * i + s
-            shift(z0 + k + 1, (s + 1) % unroll)
-            finish_even(jnp.maximum(k - 1, 0) if s == 0 else k - 1, (s - 1) % unroll)
+        for s in range(2):
+            k = 2 * i + s
+            shift(k + 1, (s + 1) % 2)
+            finish_even(jnp.maximum(k - 1, 0) if s == 0 else k - 1, (s - 1) % 2)
             faces(k, s)
         return carry
 
-    lax.fori_loop(0, count // unroll, planes, 0)
-    finish_even(count - 1, unroll - 1)
+    lax.fori_loop(0, count // 2, planes, 0)
+    finish_even(count - 1, 1)
+
+
+def xy_pass(load, side, acc, scr, z0, count, r0, tile_list, plane):
+    shift, finish_even, faces = x_parts(load, side, acc, scr, z0, 0, r0, tile_list, False)
+    shift(0, 0)
+    shift(1, 1)
+    faces(0, 0)
+    shift(2, 0)
+    finish_even(0, 0)
+    faces(1, 1)
+
+    def planes(i, carry):
+        for s in range(2):
+            k = 2 * i + s
+            shift(k + 1, (s + 1) % 2)
+            finish_even(k - 1, (s - 1) % 2)
+            faces(k, s)
+            plane(k - 2, s)
+        return carry
+
+    lax.fori_loop(1, count // 2, planes, 0)
+    finish_even(count - 1, 1)
+    plane(count - 2, 0)
+    plane(count - 1, 1)
 
 
 def from_work(work):
@@ -259,17 +291,33 @@
     lax.fori_loop(0, count, one, 0)
 
 
+NINTH, NEXT, FAR, SLAB = 128, 144, 192, 216
+
+
+def slab_planes():
+    near = [(DEEP - 3 + i if i < 3 else DEEP + 13 + i, NEXT + 8 * i, 8) for i in range(6)]
+    far = [(DEEP - 6 + i if i < 3 else DEEP + 16 + i, FAR + 4 * i, 4) for i in range(6)]
+    return near + far
+
+
 def load_rows(work, yo_ref, ye_ref, odd_y):
     def both(low, high):
-        def one(z, carry):
+        def own(i, carry):
+            for sub in range(2):
+                k = 2 * i + sub
+                z = DEEP + k
+                for h in range(2):
+                    work[h, at(z, ROW0 - 8), :] = low[h, pl.ds(8 * k, 8), :]
+                    work[h, at(z, ROW0 - 9, 1), :] = low[h, pl.ds(NINTH + k, 1), :]
+                    work[h, at(z, ROW0 + 32), :] = high[h, pl.ds(8 * k, 8), :]
+                    work[h, at(z, ROW0 + 40, 1), :] = high[h, pl.ds(NINTH + k, 1), :]
+            return carry
+
+        lax.fori_loop(0, 8, own, 0)
+        for z, row, n in slab_planes():
             for h in range(2):
-                work[h, at(z, ROW0 - 8), :] = low[h, pl.ds(8 * z, 8), :]
-                work[h, at(z, ROW0 - 9, 1), :] = low[h, pl.ds(272 + z, 1), :]
-                work[h, at(z, ROW0 + 32), :] = high[h, pl.ds(8 * z, 8), :]
-                work[h, at(z, ROW0 + 40, 1), :] = high[h, pl.ds(272 + z, 1), :]
-            return carry
-
-        lax.fori_loop(0, 34, one, 0)
+                work[h, at(z, ROW0 - n, n), :] = low[h, row : row + n, :]
+                work[h, at(z, ROW0 + 32, n), :] = high[h, row : row + n, :]
 
     @pl.when(odd_y == 0)
     def _():
@@ -340,7 +388,7 @@
     def load_clamped(h, z, r):
         return own_ref[jnp.minimum(z - DEEP, 15), h, pl.ds(r - ROW0, 8), :]
 
-    x_pass(load_clamped, side, acc, (shifted, finished), DEEP, 16, 6, WIDE, OWN_TILES, 2)
+    x_pass(load_clamped, side, acc, (shifted, finished), DEEP, 16, 6, WIDE, OWN_TILES)
 
 
 def planes_kernel(initial, own_ref, zo_ref, ze_ref, *refs):
@@ -356,7 +404,7 @@
     for z0 in (3, 25):
         if initial:
             signs(load, weight, side, z0, 6, OWN_ROWS)
-        x_pass(load, side, acc, (shifted, finished), z0, 6, z0 - 3, WIDE, OWN_TILES, 2)
+        x_pass(load, side, acc, (shifted, finished), z0, 6, z0 - 3, WIDE, OWN_TILES)
     z_pass(u, side, acc, 6, WIDE, 4, 1)
 
 
@@ -370,14 +418,16 @@
         out_ref, acc, u = refs[4:7]
         refs = refs[7:]
     first, second = refs[:2]
-    scr = refs[2:8]
-    x_scr = refs[8:10]
-    third = refs[10]
+    scr = refs[2:9]
+    x_scr = refs[9:11]
+    third = refs[11]
+    if not initial:
+        merged, sems = refs[12:14]
     odd_z, odd_y, is_first, is_last = position()
     load_rows(u, yo_ref, ye_ref, odd_y)
     edge_rows(u, 0, 34, True, is_first, is_last)
     if initial:
-        signs(from_work(u), weight, side, 3, 28, (WIDE, WIDE + 40))
+        signs(from_work(u), weight, side, 6, 22, (WIDE, WIDE + 40))
 
     def store(work, start):
         def put(h, zi, t, r, value):
@@ -397,34 +447,25 @@
     def third_stage(h, z, r, v):
         return (1.0 / 3.0) * u[h, at(z, r), :] + (2.0 / 3.0) * v
 
-    x_pass(from_work(u), side, acc, x_scr, 3, 28, 0, WIDE, (0, 5), 4)
-    z_pass(u, side, acc, 6, WIDE, 2, 0, 5)
-    y_pass(
-        u, side, weight, acc, scr, store(first, 3), lambda h, z, r, v: v, 6, WIDE, 6, 6, (1, 9, 17, 25, 33, 41)
+    z_pass(u, side, acc, 3, WIDE, 2, 0, 5, 3, True)
+    rows = (1, 9, 17, 25, 33, 41)
+    rows = rows, rows, rows + (42,)
+    plane = y_plane(u, side, weight, acc, scr, store(first, 3), lambda h, z, r, v: v, 6, WIDE, 6, 6, rows)
+    xy_pass(from_work(u), side, acc, x_scr, 3, 28, WIDE, (0, 5), plane)
+    edge_rows(first, 3, 28, False, is_first, is_last)
+    z_pass(first, side, acc, 3, ROW0 - 3, 5, fresh=True)
+    rows = tuple(range(0, 48, 8))
+    below = tuple(range(-1, 47, 8))
+    plane = y_plane(
+        first, side, weight, acc, scr, store(second, 6), second_stage, 3, ROW0 - 3, 5, 5, (rows, below, below)
     )
-    edge_rows(first, 3, 28, False, is_first, is_last)
-    x_pass(from_work(first), side, acc, x_scr, 6, 22, 0, ROW0 - 3, range(5), 2)
-    z_pass(first, side, acc, 3, ROW0 - 3, 5)
-    y_pass(
-        first, side, weight, acc, scr, store(second, 6), second_stage, 3, ROW0 - 3, 5, 5, (0, 8, 16, 24, 32, 40)
-    )
+    xy_pass(from_work(first), side, acc, x_scr, 6, 22, ROW0 - 3, range(5), plane)
     edge_rows(second, 6, 22, False, is_first, is_last)
-    x_pass(from_work(second), side, acc, x_scr, 9, 16, 0, ROW0, range(4), 2)
-    z_pass(second, side, acc, 0, ROW0, 4)
-    y_pass(
-        second,
-        side,
-        weight,
-        acc,
-        scr,
-        put_out if initial else put_third,
-        third_stage,
-        0,
-        ROW0,
-        4,
-        5,
-        (0, 8, 16, 24, 32),
-    )
+    z_pass(second, side, acc, 0, ROW0, 4, fresh=True)
+    put = put_out if initial else put_third
+    rows, below = rows[:5], below[:5]
+    plane = y_plane(second, side, weight, acc, scr, put, third_stage, 0, ROW0, 4, 5, (rows, below, below))
+    xy_pass(from_work(second), side, acc, x_scr, 9, 16, ROW0, range(4), plane)
 
     if initial:
 
@@ -438,16 +479,21 @@
         lane = lax.broadcasted_iota(jnp.int32, (8, 128), 1)
         even = (lane & 1) == 0
         half = lane >> 1
-
-        def merge(k, carry):
-            for t in range(4):
-                rows = pl.ds(k * 32 + 8 * t, 8)
-                for h in range(2):
-                    parts = [jnp.take_along_axis(third[p, rows, :], half + 64 * h, axis=1) for p in range(2)]
-                    out_ref[k, 8 * t : 8 * t + 8, 128 * h : 128 * h + 128] = jnp.where(even, *parts)
-            return carry
-
-        lax.fori_loop(0, 16, merge, 0)
+        copies = []
+        for chunk in range(4):
+            for k in range(4 * chunk, 4 * chunk + 4):
+                for t in range(4):
+                    rows = pl.ds(k * 32 + 8 * t, 8)
+                    for h in range(2):
+                        parts = [
+                            jnp.take_along_axis(third[p, rows, :], half + 64 * h, axis=1) for p in range(2)
+                        ]
+                        merged[k, 8 * t : 8 * t + 8, 128 * h : 128 * h + 128] = jnp.where(even, *parts)
+            planes = pl.ds(4 * chunk, 4)
+            copies.append(pltpu.make_async_copy(merged.at[planes], out_ref.at[planes], sems.at[chunk]))
+            copies[-1].start()
+        for copy in copies:
+            copy.wait()
 
 
 def split_kernel(own_ref, out_ref, so_ref, se_ref):
@@ -455,16 +501,13 @@
     lane = lax.broadcasted_iota(jnp.int32, (8, 128), 1)
     low = lane < 64
     twice = (lane & 63) * 2
-
-    def plane(k, carry):
-        for t in range(4):
-            v = [own_ref[k, 8 * t : 8 * t + 8, 128 * h : 128 * h + 128] for h in range(2)]
-            for p in range(2):
-                parts = [jnp.take_along_axis(x, twice + p, axis=1) for x in v]
-                out_ref[k, p, 8 * t : 8 * t + 8, :] = jnp.where(low, *parts)
-        return carry
-
-    lax.fori_loop(0, 16, plane, 0)
+    for chunk in range(4):
+        for k in range(4 * chunk, 4 * chunk + 4):
+            for t in range(4):
+                v = [own_ref[k, 8 * t : 8 * t + 8, 128 * h : 128 * h + 128] for h in range(2)]
+                for p in range(2):
+                    parts = [jnp.take_along_axis(x, twice + p, axis=1) for x in v]
+                    out_ref[k, p, 8 * t : 8 * t + 8, :] = jnp.where(low, *parts)
 
     def slabs(k, carry):
         so_ref[k] = out_ref[k + 7 * odd_z]
@@ -475,33 +518,34 @@
 
 
 def pack_kernel(own_ref, zo_ref, ze_ref, yo_ref, ye_ref):
-    odd_z = lax.rem(lax.axis_index("gz"), 2)
-    odd_y = lax.rem(lax.axis_index("gy"), 2)
-
-    def fill(out, main, extra):
-        def planes(ref, start, count):
-            def one(k, carry):
+    odd_z, odd_y, _, _ = position()
+
+    def fill(out, top, low_ref, high_ref):
+        main, ninth, short = (24, 23, 28) if top else (0, 8, 0)
+
+        def own(i, carry):
+            for sub in range(2):
+                k = 2 * i + sub
                 for h in range(2):
-                    out[h, pl.ds(8 * (start + k), 8), :] = ref[k, h, main : main + 8, :]
-                    out[h, pl.ds(272 + start + k, 1), :] = ref[k, h, extra : extra + 1, :]
-                return carry
-
-            lax.fori_loop(0, count, one, 0)
-
-        planes(own_ref, DEEP, 16)
-        planes(zo_ref, 25 * odd_z, DEEP)
-        planes(ze_ref, 25 * (1 - odd_z), DEEP)
-        out[:, 306:312, :] = jnp.zeros((2, 6, 128), f32)
-
-    @pl.when(odd_y == 0)
-    def _():
-        fill(yo_ref, 0, 8)
-        fill(ye_ref, 24, 23)
-
-    @pl.when(odd_y == 1)
-    def _():
-        fill(yo_ref, 24, 23)
-        fill(ye_ref, 0, 8)
+                    out[h, pl.ds(8 * k, 8), :] = own_ref[k, h, main : main + 8, :]
+                    out[h, pl.ds(NINTH + k, 1), :] = own_ref[k, h, ninth : ninth + 1, :]
+            return carry
+
+        lax.fori_loop(0, 8, own, 0)
+        for z, row, n in slab_planes():
+            ref, k = (low_ref, z) if z < DEEP else (high_ref, z - DEEP - 16)
+            first = main if n == 8 else short
+            for h in range(2):
+                out[h, row : row + n, :] = ref[k, h, first : first + n, :]
+
+    for z_parity in range(2):
+        for y_parity in range(2):
+
+            @pl.when((odd_z == z_parity) & (odd_y == y_parity))
+            def _(z_parity=z_parity, y_parity=y_parity):
+                low_ref, high_ref = (ze_ref, zo_ref) if z_parity else (zo_ref, ze_ref)
+                fill(yo_ref, y_parity == 1, low_ref, high_ref)
+                fill(ye_ref, y_parity == 0, low_ref, high_ref)
 
 
 def swaps(count, start, periodic):
@@ -518,28 +562,29 @@
 ACC = (2, 28 * 48, 128)
 
 
-def call(kernel, name, args, outs, scratch=(), aliases=None, cycles=1000):
-    result = pl.pallas_call(
+def call(kernel, name, args, outs, scratch=(), aliases=None, cycles=1000, hbm=()):
+    anywhere = pl.BlockSpec(memory_space=pltpu.HBM)
+    more = [pltpu.VMEM((16, 32, 256), f32), pltpu.SemaphoreType.DMA((4,))] if hbm else []
+    return pl.pallas_call(
         kernel,
         out_shape=[jax.ShapeDtypeStruct(shape, f32) for shape in outs],
-        in_specs=[VMEM] * len(args),
-        out_specs=[VMEM] * len(outs),
-        scratch_shapes=[pltpu.VMEM(shape, f32) for shape in scratch],
+        in_specs=[anywhere if ("in", i) == hbm else VMEM for i in range(len(args))],
+        out_specs=[anywhere if ("out", i) == hbm else VMEM for i in range(len(outs))],
+        scratch_shapes=[pltpu.VMEM(shape, f32) for shape in scratch] + more,
         input_output_aliases=aliases or {},
         compiler_params=pltpu.CompilerParams(vmem_limit_bytes=24 * 1024 * 1024),
         cost_estimate=pl.CostEstimate(flops=4096 * cycles, bytes_accessed=4096 * cycles, transcendentals=0),
         name=name,
     )(*args)
-    return result
 
 
 def per_device(level_set):
     n_z, n_y = lax.axis_size("gz"), lax.axis_size("gy")
     z_odd, z_even = swaps(n_z, 1, True), swaps(n_z, 0, True)
     y_odd, y_even = swaps(n_y, 1, False), swaps(n_y, 0, False)
-    split, deep, slab = (16, 2, 32, 128), (DEEP, 2, 32, 128), (2, 312, 128)
+    split, deep, slab = (16, 2, 32, 128), (DEEP, 2, 32, 128), (2, SLAB, 128)
     shifts = [(2, 5, 48, 128), (2, 2, 48, 128)]
-    rest_scratch = [WORK] * 2 + [(4, 56, 128)] * 6 + [(4, 5, 48, 128), (4, 2, 48, 128), (2, 512, 128)]
+    rest_scratch = [WORK] * 2 + [(4, 56, 128)] * 7 + shifts + [(2, 512, 128)]
     field, z_send_odd, z_send_even = call(split_kernel, "split_cells", (level_set,), [split, deep, deep])
     weight = side = None
     for step in range(STEPS):
@@ -593,6 +638,7 @@
                 rest_scratch,
                 {4: 1, 5: 2},
                 30000,
+                ("out", 0),
             )
     return field
 

time: 86 us -> 79.8 us (0.928)
  Pallas kernels: 49.9 us -> 45.7 us
  waiting for transfers between devices: 13.3 us -> 11.8 us
    pallas_call x9, Pallas kernels: 49.9 us -> 45.7 us  [call(): pl.pallas_call(kernel, out_shape=[jax.ShapeDtypeStruct(shape, f32) for sh...]
    ppermute x2, waiting for transfers between devices: 1.61 us -> 0.56 us  [per_device(): ye = lax.ppermute(y_send_even, 'gy', y_even)]
    ppermute x2, waiting for transfers between devices: 2.05 us -> 1 us  [per_device(): yo = lax.ppermute(y_send_odd, 'gy', y_odd)]
  transfers between devices with their start and end apart: 8 -> 8, of which waited for: 4 -> 4; matrix products, arithmetic and copies ran while one was open for 0% -> 0% of each run, Pallas kernels for 12% -> 13%
where the time goes in v3:
time: 79.8 us; the launch traced here: 79.6 us
  Pallas kernels  45.7 us (57%)
  starting transfers between devices  20.8 us (26%)
  waiting for transfers between devices  11.8 us (15%)
  local copies, waits for them, and re-layouts  1.04 us (1%)
    pallas_call x9, Pallas kernels, call(): pl.pallas_call(kernel, out_shape=[jax.ShapeDtypeStruct(shape, f32) for sh...  45.7 us
    ppermute x2, starting transfers between devices, per_device(): zo = lax.ppermute(z_send_odd, 'gz', z_odd)  11 us
    ppermute x2, waiting for transfers between devices, per_device(): zo = lax.ppermute(z_send_odd, 'gz', z_odd)  10.2 us
    ppermute x2, starting transfers between devices, per_device(): yo = lax.ppermute(y_send_odd, 'gy', y_odd)  9.69 us
  transfers between devices with their start and end apart: 8, of which 4 were waited for; matrix products, arithmetic and copies ran while one was open for 0% of the time, Pallas kernels for 13%

profile of v3, /device:TPU:2, one launch (start us, length us, event | category | flops | bytes accessed | tf_op | source)
XLA Modules:
  0.0 79.6 jit_solution(3007570806751154357)
XLA Ops:
  0.0 1.0 %copy-done = f32[16,32,256]{2,1,0:T(8,128)S(1)} copy-done((f32[16,32,256]{2,1,0:T(8,128)S(1)}, f32[16,32,256]{2,1,0:T(8,128)}, u32[]{:S(2)}) %copy-start) | copy-done | bytes 524312
  1.0 0.7 split_cells.1
  1.8 6.9 %collective-permute-start = (f32[9,2,32,128]{3,2,1,0:T(8,128)S(1)}, f32[9,2,32,128]{3,2,1,0:T(8,128)S(1)}, u32[]{:S(2)}, u32[]{:S(2)}) collective-permute-start(f32[9,2,32,128]{3,2,1,0:T(8,128)S(1)} %get-tuple-element.28), channel_id=1, source_target_pairs={{8,16},{16,8},{24,32},{32,24},{40,48},{48,40},{56,64},{64,56},{72,... | collective-permute-start | bytes 884744 | tf_op jit(solution)/shard_map/ppermute | solution.py:592
  8.7 0.0 collective-permute-start.1
  8.7 4.4 %collective-permute-done.zo_ref = f32[9,2,32,128]{3,2,1,0:T(8,128)S(1)} collective-permute-done((f32[9,2,32,128]{3,2,1,0:T(8,128)S(1)}, f32[9,2,32,128]{3,2,1,0:T(8,128)S(1)}, u32[]{:S(2)}, u32[]{:S(2)}) %collective-permute-start) | collective-permute-done | bytes 294944 | tf_op jit(solution)/shard_map/ppermute | solution.py:592
  13.1 0.0 collective-permute-done.1.ze_ref
  13.1 0.1 pack_rows.2
  13.3 5.8 %collective-permute-start.2 = (f32[2,216,128]{2,1,0:T(8,128)S(1)}, f32[2,216,128]{2,1,0:T(8,128)S(1)}, u32[]{:S(2)}, u32[]{:S(2)}) collective-permute-start(f32[2,216,128]{2,1,0:T(8,128)S(1)} %get-tuple-element.30), channel_id=1, source_target_pairs={{1,2},{2,1},{3,4},{4,3},{5,6},{6,5},{9,10},{10,9},{11,12},{12,11},... | collective-permute-start | bytes 663560 | tf_op jit(solution)/shard_map/ppermute | solution.py:602
  19.1 0.1 collective-permute-start.3
  19.2 1.9 %own_planes.1 = (f32[2,2176,128]{2,1,0:T(8,128)S(1)}, f32[2,2176,128]{2,1,0:T(8,128)S(1)}, f32[2,1344,128]{2,1,0:T(8,128)S(1)}) custom-call(f32[16,2,32,128]{3,2,1,0:T(8,128)S(1)} %get-tuple-element.27.own_ref), custom_call_target="tpu_custom_call" | custom-call | flops 16384000 | bytes 16384000 | tf_op jit(solution)/shard_map/own_planes/pallas_call | solution.py:568
  21.1 3.4 %ghost_planes.1 = (f32[2,2176,128]{2,1,0:T(8,128)S(1)}, f32[2,2176,128]{2,1,0:T(8,128)S(1)}, f32[2,1344,128]{2,1,0:T(8,128)S(1)}, f32[2,2176,128]{2,1,0:T(8,128)S(1)}) custom-call(f32[16,2,32,128]{3,2,1,0:T(8,128)S(1)} %get-tuple-element.27.own_ref, ...), custom_call_target="tpu_custom_call", output_to_operand_aliasing={{0}: (3, {}), {1}: (4, {}), {2}: (5, {})} | custom-call | flops 32768000 | bytes 32768000 | tf_op jit(solution)/shard_map/ghost_planes/pallas_call | solution.py:568
  24.5 0.6 collective-permute-done.3.ye_ref
  25.1 16.7 %first_step.1 = (f32[16,2,32,128]{3,2,1,0:T(8,128)S(1)}, f32[9,2,32,128]{3,2,1,0:T(8,128)S(1)}, f32[9,2,32,128]{3,2,1,0:T(8,128)S(1)}, f32[2,2176,128]{2,1,0:T(8...) custom-call(f32[2,216,128]{2,1,0:T(8,128)S(1)} %collective-permute-d, ...), custom_call_target="tpu_custom_call", output_to_operand_aliasing={{3}: (2, {}), {4}: (3, {}), {5}: (4, {}), {6}: (5, {})} | custom-call | flops 122880000 | bytes 122880000 | tf_op jit(solution)/shard_map/first_step/pallas_call | solution.py:568
  41.8 4.0 %collective-permute-start.4 = (f32[9,2,32,128]{3,2,1,0:T(8,128)S(1)}, f32[9,2,32,128]{3,2,1,0:T(8,128)S(1)}, u32[]{:S(2)}, u32[]{:S(2)}) collective-permute-start(f32[9,2,32,128]{3,2,1,0:T(8,128)S(1)} %get-tuple-element.40), channel_id=1, source_target_pairs={{8,16},{16,8},{24,32},{32,24},{40,48},{48,40},{56,64},{64,56},{72,... | collective-permute-start | bytes 884744 | tf_op jit(solution)/shard_map/ppermute | solution.py:592
  45.8 5.8 %collective-permute-done.4.zo_ref = f32[9,2,32,128]{3,2,1,0:T(8,128)S(1)} collective-permute-done((f32[9,2,32,128]{3,2,1,0:T(8,128)S(1)}, f32[9,2,32,128]{3,2,1,0:T(8,128)S(1)}, u32[]{:S(2)}, u32[]{:S(2)}) %collective-permute-start.4) | collective-permute-done | bytes 294944 | tf_op jit(solution)/shard_map/ppermute | solution.py:592
  51.7 0.0 collective-permute-done.5.ze_ref
  51.7 0.1 pack_rows.3
  51.8 3.9 %collective-permute-start.6 = (f32[2,216,128]{2,1,0:T(8,128)S(1)}, f32[2,216,128]{2,1,0:T(8,128)S(1)}, u32[]{:S(2)}, u32[]{:S(2)}) collective-permute-start(f32[2,216,128]{2,1,0:T(8,128)S(1)} %get-tuple-element.42), channel_id=1, source_target_pairs={{1,2},{2,1},{3,4},{4,3},{5,6},{6,5},{9,10},{10,9},{11,12},{12,11},... | collective-permute-start | bytes 663560 | tf_op jit(solution)/shard_map/ppermute | solution.py:602
  55.7 0.1 collective-permute-start.7
  55.8 1.7 %own_planes_next.1.refs_1_ = f32[2,1344,128]{2,1,0:T(8,128)S(1)} custom-call(f32[16,2,32,128]{3,2,1,0:T(8,128)S(1)} %get-tuple-element.39.own_ref, f32[2,2176,128]{2,1,0:T(8,128)S(1)} %get-tuple-element.45.refs_0_.refs_1_), custom_call_target="tpu_custom_call" | custom-call | flops 16384000 | bytes 16384000 | tf_op jit(solution)/shard_map/own_planes_next/pallas_call | solution.py:568
  57.5 3.2 %ghost_planes_next.1 = (f32[2,1344,128]{2,1,0:T(8,128)S(1)}, f32[2,2176,128]{2,1,0:T(8,128)S(1)}) custom-call(f32[16,2,32,128]{3,2,1,0:T(8,128)S(1)} %get-tuple-element.39.own_ref, f32[9,2,32,128]{3,2,1,0:T(8,128)S(1)} %collective-permute-done.4.zo_ref, f32[9,2,32,128]{3,2,1,0:T(8,128)S(1)} %collective-permute-done.5.ze_ref, ...), custom_call_target="tpu_custom_call", output_to_operand_aliasing={{0}: (4, {})} | custom-call | flops 32768000 | bytes 32768000 | tf_op jit(solution)/shard_map/ghost_planes_next/pallas_call | solution.py:568
  60.7 1.0 %collective-permute-done.6.yo_ref = f32[2,216,128]{2,1,0:T(8,128)S(1)} collective-permute-done((f32[2,216,128]{2,1,0:T(8,128)S(1)}, f32[2,216,128]{2,1,0:T(8,128)S(1)}, u32[]{:S(2)}, u32[]{:S(2)}) %collective-permute-start.6) | collective-permute-done | bytes 221216 | tf_op jit(solution)/shard_map/ppermute | solution.py:602
  61.7 0.0 collective-permute-done.7.ye_ref
  61.7 17.7 %next_step.1 = (f32[16,32,256]{2,1,0:T(8,128)}, f32[2,1344,128]{2,1,0:T(8,128)S(1)}, f32[2,2176,128]{2,1,0:T(8,128)S(1)}) custom-call(f32[2,216,128]{2,1,0:T(8,128)S(1)} %collective-permute-done.6.yo_ref, f32[2,216,128]{2,1,0:T(8,128)S(1)} %collective-permute-done.7.ye_ref, ...), custom_call_target="tpu_custom_call", output_to_operand_aliasing={{1}: (4, {}), {2}: (5, {})} | custom-call | flops 122880000 | bytes 122880000 | tf_op jit(solution)/shard_map/next_step/pallas_call | solution.py:568
  (3 shorter events, 0.0 us)
Async XLA Ops:
  0.0 1.0 %copy-start = (f32[16,32,256]{2,1,0:T(8,128)S(1)}, f32[16,32,256]{2,1,0:T(8,128)}, u32[]{:S(2)}) copy-start(f32[16,32,256]{2,1,0:T(8,128)} %own_ref.1) | copy-start | bytes 1572868
  1.8 11.4 %collective-permute-start = (f32[9,2,32,128]{3,2,1,0:T(8,128)S(1)}, f32[9,2,32,128]{3,2,1,0:T(8,128)S(1)}, u32[]{:S(2)}, u32[]{:S(2)}) collective-permute-start(f32[9,2,32,128]{3,2,1,0:T(8,128)S(1)} %get-tuple-element.28), channel_id=1, source_target_pairs={{8,16},{16,8},{24,32},{32,24},{40,48},{48,40},{56,64},{64,56},{72,... | collective-permute-start | bytes 884744 | tf_op jit(solution)/shard_map/ppermute | solution.py:592
  8.7 4.4 %collective-permute-start.1 = (f32[9,2,32,128]{3,2,1,0:T(8,128)S(1)}, f32[9,2,32,128]{3,2,1,0:T(8,128)S(1)}, u32[]{:S(2)}, u32[]{:S(2)}) collective-permute-start(f32[9,2,32,128]{3,2,1,0:T(8,128)S(1)} %get-tuple-element.29), channel_id=1, source_target_pairs={{0,8},{8,0},{16,24},{24,16},{32,40},{40,32},{48,56},{56,48},{64,72... | collective-permute-start | bytes 884744 | tf_op jit(solution)/shard_map/ppermute | solution.py:593
  13.3 11.2 %collective-permute-start.2 = (f32[2,216,128]{2,1,0:T(8,128)S(1)}, f32[2,216,128]{2,1,0:T(8,128)S(1)}, u32[]{:S(2)}, u32[]{:S(2)}) collective-permute-start(f32[2,216,128]{2,1,0:T(8,128)S(1)} %get-tuple-element.30), channel_id=1, source_target_pairs={{1,2},{2,1},{3,4},{4,3},{5,6},{6,5},{9,10},{10,9},{11,12},{12,11},... | collective-permute-start | bytes 663560 | tf_op jit(solution)/shard_map/ppermute | solution.py:602
  19.1 6.0 %collective-permute-start.3 = (f32[2,216,128]{2,1,0:T(8,128)S(1)}, f32[2,216,128]{2,1,0:T(8,128)S(1)}, u32[]{:S(2)}, u32[]{:S(2)}) collective-permute-start(f32[2,216,128]{2,1,0:T(8,128)S(1)} %get-tuple-element.31), channel_id=1, source_target_pairs={{0,1},{1,0},{2,3},{3,2},{4,5},{5,4},{6,7},{7,6},{8,9},{9,8},{10,11... | collective-permute-start | bytes 663560 | tf_op jit(solution)/shard_map/ppermute | solution.py:603
  41.8 9.8 %collective-permute-start.4 = (f32[9,2,32,128]{3,2,1,0:T(8,128)S(1)}, f32[9,2,32,128]{3,2,1,0:T(8,128)S(1)}, u32[]{:S(2)}, u32[]{:S(2)}) collective-permute-start(f32[9,2,32,128]{3,2,1,0:T(8,128)S(1)} %get-tuple-element.40), channel_id=1, source_target_pairs={{8,16},{16,8},{24,32},{32,24},{40,48},{48,40},{56,64},{64,56},{72,... | collective-permute-start | bytes 884744 | tf_op jit(solution)/shard_map/ppermute | solution.py:592
  45.8 5.8 %collective-permute-start.5 = (f32[9,2,32,128]{3,2,1,0:T(8,128)S(1)}, f32[9,2,32,128]{3,2,1,0:T(8,128)S(1)}, u32[]{:S(2)}, u32[]{:S(2)}) collective-permute-start(f32[9,2,32,128]{3,2,1,0:T(8,128)S(1)} %get-tuple-element.41), channel_id=1, source_target_pairs={{0,8},{8,0},{16,24},{24,16},{32,40},{40,32},{48,56},{56,48},{64,72... | collective-permute-start | bytes 884744 | tf_op jit(solution)/shard_map/ppermute | solution.py:593
  51.8 9.9 %collective-permute-start.6 = (f32[2,216,128]{2,1,0:T(8,128)S(1)}, f32[2,216,128]{2,1,0:T(8,128)S(1)}, u32[]{:S(2)}, u32[]{:S(2)}) collective-permute-start(f32[2,216,128]{2,1,0:T(8,128)S(1)} %get-tuple-element.42), channel_id=1, source_target_pairs={{1,2},{2,1},{3,4},{4,3},{5,6},{6,5},{9,10},{10,9},{11,12},{12,11},... | collective-permute-start | bytes 663560 | tf_op jit(solution)/shard_map/ppermute | solution.py:602
  55.7 6.0 %collective-permute-start.7 = (f32[2,216,128]{2,1,0:T(8,128)S(1)}, f32[2,216,128]{2,1,0:T(8,128)S(1)}, u32[]{:S(2)}, u32[]{:S(2)}) collective-permute-start(f32[2,216,128]{2,1,0:T(8,128)S(1)} %get-tuple-element.43), channel_id=1, source_target_pairs={{0,1},{1,0},{2,3},{3,2},{4,5},{5,4},{6,7},{7,6},{8,9},{9,8},{10,11... | collective-permute-start | bytes 663560 | tf_op jit(solution)/shard_map/ppermute | solution.py:603

commit v4 on v3

--- a/solution.py
+++ b/solution.py
@@ -248,7 +248,7 @@
     finish_even(count - 1, 1)
 
 
-def xy_pass(load, side, acc, scr, z0, count, r0, tile_list, plane):
+def xy_pass(load, side, acc, scr, z0, count, r0, tile_list, plane, after=None, tail=None):
     shift, finish_even, faces = x_parts(load, side, acc, scr, z0, 0, r0, tile_list, False)
     shift(0, 0)
     shift(1, 1)
@@ -264,12 +264,21 @@
             finish_even(k - 1, (s - 1) % 2)
             faces(k, s)
             plane(k - 2, s)
+            if after is not None:
+                after(jnp.maximum(k - 4, 0))
         return carry
 
     lax.fori_loop(1, count // 2, planes, 0)
+    if after is not None:
+        tail()
+        after(count - 4)
+        after(count - 3)
     finish_even(count - 1, 1)
     plane(count - 2, 0)
     plane(count - 1, 1)
+    if after is not None:
+        after(count - 2)
+        after(count - 1)
 
 
 def from_work(work):
@@ -465,9 +474,9 @@
     put = put_out if initial else put_third
     rows, below = rows[:5], below[:5]
     plane = y_plane(second, side, weight, acc, scr, put, third_stage, 0, ROW0, 4, 5, (rows, below, below))
-    xy_pass(from_work(second), side, acc, x_scr, 9, 16, ROW0, range(4), plane)
 
     if initial:
+        xy_pass(from_work(second), side, acc, x_scr, 9, 16, ROW0, range(4), plane)
 
         def slabs(k, carry):
             so_ref[k] = out_ref[k + 7 * odd_z]
@@ -479,19 +488,25 @@
         lane = lax.broadcasted_iota(jnp.int32, (8, 128), 1)
         even = (lane & 1) == 0
         half = lane >> 1
+
+        def merge(k):
+            for t in range(4):
+                rows = pl.ds(k * 32 + 8 * t, 8)
+                for h in range(2):
+                    parts = [jnp.take_along_axis(third[p, rows, :], half + 64 * h, axis=1) for p in range(2)]
+                    merged[k, 8 * t : 8 * t + 8, 128 * h : 128 * h + 128] = jnp.where(even, *parts)
+
         copies = []
         for chunk in range(4):
-            for k in range(4 * chunk, 4 * chunk + 4):
-                for t in range(4):
-                    rows = pl.ds(k * 32 + 8 * t, 8)
-                    for h in range(2):
-                        parts = [
-                            jnp.take_along_axis(third[p, rows, :], half + 64 * h, axis=1) for p in range(2)
-                        ]
-                        merged[k, 8 * t : 8 * t + 8, 128 * h : 128 * h + 128] = jnp.where(even, *parts)
             planes = pl.ds(4 * chunk, 4)
             copies.append(pltpu.make_async_copy(merged.at[planes], out_ref.at[planes], sems.at[chunk]))
-            copies[-1].start()
+
+        def tail():
+            for copy in copies[:3]:
+                copy.start()
+
+        xy_pass(from_work(second), side, acc, x_scr, 9, 16, ROW0, range(4), plane, merge, tail)
+        copies[3].start()
         for copy in copies:
             copy.wait()
 

time: 79.8 us -> 79.2 us (level)
  no operation moved by 1% of the time
where the time goes in v4:
time: 79.2 us; the launch traced here: 79 us
  Pallas kernels  45.2 us (57%)
  starting transfers between devices  20.8 us (26%)
  waiting for transfers between devices  11.8 us (15%)
  local copies, waits for them, and re-layouts  1.04 us (1%)
    pallas_call x9, Pallas kernels, call(): pl.pallas_call(kernel, out_shape=[jax.ShapeDtypeStruct(shape, f32) for sh...  45.2 us
    ppermute x2, starting transfers between devices, per_device(): zo = lax.ppermute(z_send_odd, 'gz', z_odd)  11 us
    ppermute x2, waiting for transfers between devices, per_device(): zo = lax.ppermute(z_send_odd, 'gz', z_odd)  10.2 us
    ppermute x2, starting transfers between devices, per_device(): yo = lax.ppermute(y_send_odd, 'gy', y_odd)  9.69 us
  transfers between devices with their start and end apart: 8, of which 4 were waited for; matrix products, arithmetic and copies ran while one was open for 0% of the time, Pallas kernels for 13%

profile of v4, /device:TPU:2, one launch (start us, length us, event | category | flops | bytes accessed | tf_op | source)
XLA Modules:
  0.0 79.0 jit_solution(6799657809242703495)
XLA Ops:
  0.0 1.0 %copy-done = f32[16,32,256]{2,1,0:T(8,128)S(1)} copy-done((f32[16,32,256]{2,1,0:T(8,128)S(1)}, f32[16,32,256]{2,1,0:T(8,128)}, u32[]{:S(2)}) %copy-start) | copy-done | bytes 524312
  1.0 0.7 split_cells.1
  1.8 6.9 %collective-permute-start = (f32[9,2,32,128]{3,2,1,0:T(8,128)S(1)}, f32[9,2,32,128]{3,2,1,0:T(8,128)S(1)}, u32[]{:S(2)}, u32[]{:S(2)}) collective-permute-start(f32[9,2,32,128]{3,2,1,0:T(8,128)S(1)} %get-tuple-element.28), channel_id=1, source_target_pairs={{8,16},{16,8},{24,32},{32,24},{40,48},{48,40},{56,64},{64,56},{72,... | collective-permute-start | bytes 884744 | tf_op jit(solution)/shard_map/ppermute | solution.py:607
  8.7 0.0 collective-permute-start.1
  8.7 4.4 %collective-permute-done.zo_ref = f32[9,2,32,128]{3,2,1,0:T(8,128)S(1)} collective-permute-done((f32[9,2,32,128]{3,2,1,0:T(8,128)S(1)}, f32[9,2,32,128]{3,2,1,0:T(8,128)S(1)}, u32[]{:S(2)}, u32[]{:S(2)}) %collective-permute-start) | collective-permute-done | bytes 294944 | tf_op jit(solution)/shard_map/ppermute | solution.py:607
  13.1 0.0 collective-permute-done.1.ze_ref
  13.1 0.1 pack_rows.2
  13.3 5.8 %collective-permute-start.2 = (f32[2,216,128]{2,1,0:T(8,128)S(1)}, f32[2,216,128]{2,1,0:T(8,128)S(1)}, u32[]{:S(2)}, u32[]{:S(2)}) collective-permute-start(f32[2,216,128]{2,1,0:T(8,128)S(1)} %get-tuple-element.30), channel_id=1, source_target_pairs={{1,2},{2,1},{3,4},{4,3},{5,6},{6,5},{9,10},{10,9},{11,12},{12,11},... | collective-permute-start | bytes 663560 | tf_op jit(solution)/shard_map/ppermute | solution.py:617
  19.1 0.1 collective-permute-start.3
  19.2 1.9 %own_planes.1 = (f32[2,2176,128]{2,1,0:T(8,128)S(1)}, f32[2,2176,128]{2,1,0:T(8,128)S(1)}, f32[2,1344,128]{2,1,0:T(8,128)S(1)}) custom-call(f32[16,2,32,128]{3,2,1,0:T(8,128)S(1)} %get-tuple-element.27.own_ref), custom_call_target="tpu_custom_call" | custom-call | flops 16384000 | bytes 16384000 | tf_op jit(solution)/shard_map/own_planes/pallas_call | solution.py:583
  21.1 3.4 %ghost_planes.1 = (f32[2,2176,128]{2,1,0:T(8,128)S(1)}, f32[2,2176,128]{2,1,0:T(8,128)S(1)}, f32[2,1344,128]{2,1,0:T(8,128)S(1)}, f32[2,2176,128]{2,1,0:T(8,128)S(1)}) custom-call(f32[16,2,32,128]{3,2,1,0:T(8,128)S(1)} %get-tuple-element.27.own_ref, ...), custom_call_target="tpu_custom_call", output_to_operand_aliasing={{0}: (3, {}), {1}: (4, {}), {2}: (5, {})} | custom-call | flops 32768000 | bytes 32768000 | tf_op jit(solution)/shard_map/ghost_planes/pallas_call | solution.py:583
  24.5 0.6 collective-permute-done.3.ye_ref
  25.1 16.7 %first_step.1 = (f32[16,2,32,128]{3,2,1,0:T(8,128)S(1)}, f32[9,2,32,128]{3,2,1,0:T(8,128)S(1)}, f32[9,2,32,128]{3,2,1,0:T(8,128)S(1)}, f32[2,2176,128]{2,1,0:T(8...) custom-call(f32[2,216,128]{2,1,0:T(8,128)S(1)} %collective-permute-d, ...), custom_call_target="tpu_custom_call", output_to_operand_aliasing={{3}: (2, {}), {4}: (3, {}), {5}: (4, {}), {6}: (5, {})} | custom-call | flops 122880000 | bytes 122880000 | tf_op jit(solution)/shard_map/first_step/pallas_call | solution.py:583
  41.8 4.0 %collective-permute-start.4 = (f32[9,2,32,128]{3,2,1,0:T(8,128)S(1)}, f32[9,2,32,128]{3,2,1,0:T(8,128)S(1)}, u32[]{:S(2)}, u32[]{:S(2)}) collective-permute-start(f32[9,2,32,128]{3,2,1,0:T(8,128)S(1)} %get-tuple-element.40), channel_id=1, source_target_pairs={{8,16},{16,8},{24,32},{32,24},{40,48},{48,40},{56,64},{64,56},{72,... | collective-permute-start | bytes 884744 | tf_op jit(solution)/shard_map/ppermute | solution.py:607
  45.8 5.8 %collective-permute-done.4.zo_ref = f32[9,2,32,128]{3,2,1,0:T(8,128)S(1)} collective-permute-done((f32[9,2,32,128]{3,2,1,0:T(8,128)S(1)}, f32[9,2,32,128]{3,2,1,0:T(8,128)S(1)}, u32[]{:S(2)}, u32[]{:S(2)}) %collective-permute-start.4) | collective-permute-done | bytes 294944 | tf_op jit(solution)/shard_map/ppermute | solution.py:607
  51.7 0.0 collective-permute-done.5.ze_ref
  51.7 0.1 pack_rows.3
  51.8 3.9 %collective-permute-start.6 = (f32[2,216,128]{2,1,0:T(8,128)S(1)}, f32[2,216,128]{2,1,0:T(8,128)S(1)}, u32[]{:S(2)}, u32[]{:S(2)}) collective-permute-start(f32[2,216,128]{2,1,0:T(8,128)S(1)} %get-tuple-element.42), channel_id=1, source_target_pairs={{1,2},{2,1},{3,4},{4,3},{5,6},{6,5},{9,10},{10,9},{11,12},{12,11},... | collective-permute-start | bytes 663560 | tf_op jit(solution)/shard_map/ppermute | solution.py:617
  55.7 0.1 collective-permute-start.7
  55.8 1.7 %own_planes_next.1.refs_1_ = f32[2,1344,128]{2,1,0:T(8,128)S(1)} custom-call(f32[16,2,32,128]{3,2,1,0:T(8,128)S(1)} %get-tuple-element.39.own_ref, f32[2,2176,128]{2,1,0:T(8,128)S(1)} %get-tuple-element.45.refs_0_.refs_1_), custom_call_target="tpu_custom_call" | custom-call | flops 16384000 | bytes 16384000 | tf_op jit(solution)/shard_map/own_planes_next/pallas_call | solution.py:583
  57.5 3.2 %ghost_planes_next.1 = (f32[2,1344,128]{2,1,0:T(8,128)S(1)}, f32[2,2176,128]{2,1,0:T(8,128)S(1)}) custom-call(f32[16,2,32,128]{3,2,1,0:T(8,128)S(1)} %get-tuple-element.39.own_ref, f32[9,2,32,128]{3,2,1,0:T(8,128)S(1)} %collective-permute-done.4.zo_ref, f32[9,2,32,128]{3,2,1,0:T(8,128)S(1)} %collective-permute-done.5.ze_ref, ...), custom_call_target="tpu_custom_call", output_to_operand_aliasing={{0}: (4, {})} | custom-call | flops 32768000 | bytes 32768000 | tf_op jit(solution)/shard_map/ghost_planes_next/pallas_call | solution.py:583
  60.7 1.0 %collective-permute-done.6.yo_ref = f32[2,216,128]{2,1,0:T(8,128)S(1)} collective-permute-done((f32[2,216,128]{2,1,0:T(8,128)S(1)}, f32[2,216,128]{2,1,0:T(8,128)S(1)}, u32[]{:S(2)}, u32[]{:S(2)}) %collective-permute-start.6) | collective-permute-done | bytes 221216 | tf_op jit(solution)/shard_map/ppermute | solution.py:617
  61.7 0.0 collective-permute-done.7.ye_ref
  61.7 17.3 %next_step.1 = (f32[16,32,256]{2,1,0:T(8,128)}, f32[2,1344,128]{2,1,0:T(8,128)S(1)}, f32[2,2176,128]{2,1,0:T(8,128)S(1)}) custom-call(f32[2,216,128]{2,1,0:T(8,128)S(1)} %collective-permute-done.6.yo_ref, f32[2,216,128]{2,1,0:T(8,128)S(1)} %collective-permute-done.7.ye_ref, ...), custom_call_target="tpu_custom_call", output_to_operand_aliasing={{1}: (4, {}), {2}: (5, {})} | custom-call | flops 122880000 | bytes 122880000 | tf_op jit(solution)/shard_map/next_step/pallas_call | solution.py:583
  (3 shorter events, 0.0 us)
Async XLA Ops:
  0.0 1.0 %copy-start = (f32[16,32,256]{2,1,0:T(8,128)S(1)}, f32[16,32,256]{2,1,0:T(8,128)}, u32[]{:S(2)}) copy-start(f32[16,32,256]{2,1,0:T(8,128)} %own_ref.1) | copy-start | bytes 1572868
  1.8 11.4 %collective-permute-start = (f32[9,2,32,128]{3,2,1,0:T(8,128)S(1)}, f32[9,2,32,128]{3,2,1,0:T(8,128)S(1)}, u32[]{:S(2)}, u32[]{:S(2)}) collective-permute-start(f32[9,2,32,128]{3,2,1,0:T(8,128)S(1)} %get-tuple-element.28), channel_id=1, source_target_pairs={{8,16},{16,8},{24,32},{32,24},{40,48},{48,40},{56,64},{64,56},{72,... | collective-permute-start | bytes 884744 | tf_op jit(solution)/shard_map/ppermute | solution.py:607
  8.7 4.4 %collective-permute-start.1 = (f32[9,2,32,128]{3,2,1,0:T(8,128)S(1)}, f32[9,2,32,128]{3,2,1,0:T(8,128)S(1)}, u32[]{:S(2)}, u32[]{:S(2)}) collective-permute-start(f32[9,2,32,128]{3,2,1,0:T(8,128)S(1)} %get-tuple-element.29), channel_id=1, source_target_pairs={{0,8},{8,0},{16,24},{24,16},{32,40},{40,32},{48,56},{56,48},{64,72... | collective-permute-start | bytes 884744 | tf_op jit(solution)/shard_map/ppermute | solution.py:608
  13.3 11.2 %collective-permute-start.2 = (f32[2,216,128]{2,1,0:T(8,128)S(1)}, f32[2,216,128]{2,1,0:T(8,128)S(1)}, u32[]{:S(2)}, u32[]{:S(2)}) collective-permute-start(f32[2,216,128]{2,1,0:T(8,128)S(1)} %get-tuple-element.30), channel_id=1, source_target_pairs={{1,2},{2,1},{3,4},{4,3},{5,6},{6,5},{9,10},{10,9},{11,12},{12,11},... | collective-permute-start | bytes 663560 | tf_op jit(solution)/shard_map/ppermute | solution.py:617
  19.1 6.0 %collective-permute-start.3 = (f32[2,216,128]{2,1,0:T(8,128)S(1)}, f32[2,216,128]{2,1,0:T(8,128)S(1)}, u32[]{:S(2)}, u32[]{:S(2)}) collective-permute-start(f32[2,216,128]{2,1,0:T(8,128)S(1)} %get-tuple-element.31), channel_id=1, source_target_pairs={{0,1},{1,0},{2,3},{3,2},{4,5},{5,4},{6,7},{7,6},{8,9},{9,8},{10,11... | collective-permute-start | bytes 663560 | tf_op jit(solution)/shard_map/ppermute | solution.py:618
  41.8 9.8 %collective-permute-start.4 = (f32[9,2,32,128]{3,2,1,0:T(8,128)S(1)}, f32[9,2,32,128]{3,2,1,0:T(8,128)S(1)}, u32[]{:S(2)}, u32[]{:S(2)}) collective-permute-start(f32[9,2,32,128]{3,2,1,0:T(8,128)S(1)} %get-tuple-element.40), channel_id=1, source_target_pairs={{8,16},{16,8},{24,32},{32,24},{40,48},{48,40},{56,64},{64,56},{72,... | collective-permute-start | bytes 884744 | tf_op jit(solution)/shard_map/ppermute | solution.py:607
  45.8 5.8 %collective-permute-start.5 = (f32[9,2,32,128]{3,2,1,0:T(8,128)S(1)}, f32[9,2,32,128]{3,2,1,0:T(8,128)S(1)}, u32[]{:S(2)}, u32[]{:S(2)}) collective-permute-start(f32[9,2,32,128]{3,2,1,0:T(8,128)S(1)} %get-tuple-element.41), channel_id=1, source_target_pairs={{0,8},{8,0},{16,24},{24,16},{32,40},{40,32},{48,56},{56,48},{64,72... | collective-permute-start | bytes 884744 | tf_op jit(solution)/shard_map/ppermute | solution.py:608
  51.8 9.9 %collective-permute-start.6 = (f32[2,216,128]{2,1,0:T(8,128)S(1)}, f32[2,216,128]{2,1,0:T(8,128)S(1)}, u32[]{:S(2)}, u32[]{:S(2)}) collective-permute-start(f32[2,216,128]{2,1,0:T(8,128)S(1)} %get-tuple-element.42), channel_id=1, source_target_pairs={{1,2},{2,1},{3,4},{4,3},{5,6},{6,5},{9,10},{10,9},{11,12},{12,11},... | collective-permute-start | bytes 663560 | tf_op jit(solution)/shard_map/ppermute | solution.py:617
  55.7 6.0 %collective-permute-start.7 = (f32[2,216,128]{2,1,0:T(8,128)S(1)}, f32[2,216,128]{2,1,0:T(8,128)S(1)}, u32[]{:S(2)}, u32[]{:S(2)}) collective-permute-start(f32[2,216,128]{2,1,0:T(8,128)S(1)} %get-tuple-element.43), channel_id=1, source_target_pairs={{0,1},{1,0},{2,3},{3,2},{4,5},{5,4},{6,7},{7,6},{8,9},{9,8},{10,11... | collective-permute-start | bytes 663560 | tf_op jit(solution)/shard_map/ppermute | solution.py:618

commit v5 on v4

--- a/solution.py
+++ b/solution.py
@@ -291,13 +291,16 @@
 
 
 def load_planes(work, ref, start, count):
-    def one(k, carry):
-        for t in range(4):
-            for h in range(2):
-                work[h, at(start + k, ROW0 + 8 * t), :] = ref[k, h, 8 * t : 8 * t + 8, :]
+    step = 4 if count % 4 == 0 else 3
+
+    def some(i, carry):
+        for k in (step * i + sub for sub in range(step)):
+            for t in range(4):
+                for h in range(2):
+                    work[h, at(start + k, ROW0 + 8 * t), :] = ref[k, h, 8 * t : 8 * t + 8, :]
         return carry
 
-    lax.fori_loop(0, count, one, 0)
+    lax.fori_loop(0, count // step, some, 0)
 
 
 NINTH, NEXT, FAR, SLAB = 128, 144, 192, 216
@@ -338,16 +341,16 @@
 
 
 def signs(load, weight, side, z0, count, row_list):
-    def one(k, carry):
-        z = z0 + k
-        for h in range(2):
-            for r in row_list:
-                v = load(h, z, r)
-                weight[h, at(z, r), :] = (-TAU) * (v * lax.rsqrt(v * v + 1.0))
-                side[h, at(z, r), :] = jnp.where(v >= 0.0, 1.0, -1.0)
+    def two(i, carry):
+        for z in (z0 + 2 * i, z0 + 2 * i + 1):
+            for h in range(2):
+                for r in row_list:
+                    v = load(h, z, r)
+                    weight[h, at(z, r), :] = (-TAU) * (v * lax.rsqrt(v * v + 1.0))
+                    side[h, at(z, r), :] = jnp.where(v >= 0.0, 1.0, -1.0)
         return carry
 
-    lax.fori_loop(0, count, one, 0)
+    lax.fori_loop(0, count // 2, two, 0)
 
 
 def edge_rows(work, start, count, far, is_first, is_last):

time: 79.2 us -> 79.1 us (level)
  no operation moved by 1% of the time
where the time goes in v5:
time: 79.1 us; the launch traced here: 78.9 us
  Pallas kernels  44.8 us (57%)
  starting transfers between devices  20.7 us (26%)
  waiting for transfers between devices  12.3 us (16%)
  local copies, waits for them, and re-layouts  1.04 us (1%)
    pallas_call x9, Pallas kernels, call(): pl.pallas_call(kernel, out_shape=[jax.ShapeDtypeStruct(shape, f32) for sh...  44.8 us
    ppermute x2, starting transfers between devices, per_device(): zo = lax.ppermute(z_send_odd, 'gz', z_odd)  10.8 us
    ppermute x2, waiting for transfers between devices, per_device(): zo = lax.ppermute(z_send_odd, 'gz', z_odd)  10.4 us
    ppermute x2, starting transfers between devices, per_device(): yo = lax.ppermute(y_send_odd, 'gy', y_odd)  9.69 us
  transfers between devices with their start and end apart: 8, of which 4 were waited for; matrix products, arithmetic and copies ran while one was open for 0% of the time, Pallas kernels for 13%

profile of v5, /device:TPU:2, one launch (start us, length us, event | category | flops | bytes accessed | tf_op | source)
XLA Modules:
  0.0 78.9 jit_solution(6421149672846425952)
XLA Ops:
  0.0 1.0 %copy-done = f32[16,32,256]{2,1,0:T(8,128)S(1)} copy-done((f32[16,32,256]{2,1,0:T(8,128)S(1)}, f32[16,32,256]{2,1,0:T(8,128)}, u32[]{:S(2)}) %copy-start) | copy-done | bytes 524312
  1.0 0.7 split_cells.1
  1.8 6.9 %collective-permute-start = (f32[9,2,32,128]{3,2,1,0:T(8,128)S(1)}, f32[9,2,32,128]{3,2,1,0:T(8,128)S(1)}, u32[]{:S(2)}, u32[]{:S(2)}) collective-permute-start(f32[9,2,32,128]{3,2,1,0:T(8,128)S(1)} %get-tuple-element.28), channel_id=1, source_target_pairs={{8,16},{16,8},{24,32},{32,24},{40,48},{48,40},{56,64},{64,56},{72,... | collective-permute-start | bytes 884744 | tf_op jit(solution)/shard_map/ppermute | solution.py:610
  8.7 0.0 collective-permute-start.1
  8.7 4.4 %collective-permute-done.zo_ref = f32[9,2,32,128]{3,2,1,0:T(8,128)S(1)} collective-permute-done((f32[9,2,32,128]{3,2,1,0:T(8,128)S(1)}, f32[9,2,32,128]{3,2,1,0:T(8,128)S(1)}, u32[]{:S(2)}, u32[]{:S(2)}) %collective-permute-start) | collective-permute-done | bytes 294944 | tf_op jit(solution)/shard_map/ppermute | solution.py:610
  13.1 0.0 collective-permute-done.1.ze_ref
  13.1 0.1 pack_rows.2
  13.3 5.8 %collective-permute-start.2 = (f32[2,216,128]{2,1,0:T(8,128)S(1)}, f32[2,216,128]{2,1,0:T(8,128)S(1)}, u32[]{:S(2)}, u32[]{:S(2)}) collective-permute-start(f32[2,216,128]{2,1,0:T(8,128)S(1)} %get-tuple-element.30), channel_id=1, source_target_pairs={{1,2},{2,1},{3,4},{4,3},{5,6},{6,5},{9,10},{10,9},{11,12},{12,11},... | collective-permute-start | bytes 663560 | tf_op jit(solution)/shard_map/ppermute | solution.py:620
  19.1 0.1 collective-permute-start.3
  19.2 1.9 %own_planes.1 = (f32[2,2176,128]{2,1,0:T(8,128)S(1)}, f32[2,2176,128]{2,1,0:T(8,128)S(1)}, f32[2,1344,128]{2,1,0:T(8,128)S(1)}) custom-call(f32[16,2,32,128]{3,2,1,0:T(8,128)S(1)} %get-tuple-element.27.own_ref), custom_call_target="tpu_custom_call" | custom-call | flops 16384000 | bytes 16384000 | tf_op jit(solution)/shard_map/own_planes/pallas_call | solution.py:586
  21.1 3.3 %ghost_planes.1 = (f32[2,2176,128]{2,1,0:T(8,128)S(1)}, f32[2,2176,128]{2,1,0:T(8,128)S(1)}, f32[2,1344,128]{2,1,0:T(8,128)S(1)}, f32[2,2176,128]{2,1,0:T(8,128)S(1)}) custom-call(f32[16,2,32,128]{3,2,1,0:T(8,128)S(1)} %get-tuple-element.27.own_ref, ...), custom_call_target="tpu_custom_call", output_to_operand_aliasing={{0}: (3, {}), {1}: (4, {}), {2}: (5, {})} | custom-call | flops 32768000 | bytes 32768000 | tf_op jit(solution)/shard_map/ghost_planes/pallas_call | solution.py:586
  24.3 0.0 collective-permute-done.2.yo_ref
  24.3 0.8 collective-permute-done.3.ye_ref
  25.1 16.6 %first_step.1 = (f32[16,2,32,128]{3,2,1,0:T(8,128)S(1)}, f32[9,2,32,128]{3,2,1,0:T(8,128)S(1)}, f32[9,2,32,128]{3,2,1,0:T(8,128)S(1)}, f32[2,2176,128]{2,1,0:T(8...) custom-call(f32[2,216,128]{2,1,0:T(8,128)S(1)} %collective-permute-d, ...), custom_call_target="tpu_custom_call", output_to_operand_aliasing={{3}: (2, {}), {4}: (3, {}), {5}: (4, {}), {6}: (5, {})} | custom-call | flops 122880000 | bytes 122880000 | tf_op jit(solution)/shard_map/first_step/pallas_call | solution.py:586
  41.7 3.8 %collective-permute-start.4 = (f32[9,2,32,128]{3,2,1,0:T(8,128)S(1)}, f32[9,2,32,128]{3,2,1,0:T(8,128)S(1)}, u32[]{:S(2)}, u32[]{:S(2)}) collective-permute-start(f32[9,2,32,128]{3,2,1,0:T(8,128)S(1)} %get-tuple-element.40), channel_id=1, source_target_pairs={{8,16},{16,8},{24,32},{32,24},{40,48},{48,40},{56,64},{64,56},{72,... | collective-permute-start | bytes 884744 | tf_op jit(solution)/shard_map/ppermute | solution.py:610
  45.5 0.0 collective-permute-start.5
  45.5 6.0 %collective-permute-done.4.zo_ref = f32[9,2,32,128]{3,2,1,0:T(8,128)S(1)} collective-permute-done((f32[9,2,32,128]{3,2,1,0:T(8,128)S(1)}, f32[9,2,32,128]{3,2,1,0:T(8,128)S(1)}, u32[]{:S(2)}, u32[]{:S(2)}) %collective-permute-start.4) | collective-permute-done | bytes 294944 | tf_op jit(solution)/shard_map/ppermute | solution.py:610
  51.5 0.1 pack_rows.3
  51.7 3.9 %collective-permute-start.6 = (f32[2,216,128]{2,1,0:T(8,128)S(1)}, f32[2,216,128]{2,1,0:T(8,128)S(1)}, u32[]{:S(2)}, u32[]{:S(2)}) collective-permute-start(f32[2,216,128]{2,1,0:T(8,128)S(1)} %get-tuple-element.42), channel_id=1, source_target_pairs={{1,2},{2,1},{3,4},{4,3},{5,6},{6,5},{9,10},{10,9},{11,12},{12,11},... | collective-permute-start | bytes 663560 | tf_op jit(solution)/shard_map/ppermute | solution.py:620
  55.6 0.1 collective-permute-start.7
  55.7 1.7 %own_planes_next.1.refs_1_ = f32[2,1344,128]{2,1,0:T(8,128)S(1)} custom-call(f32[16,2,32,128]{3,2,1,0:T(8,128)S(1)} %get-tuple-element.39.own_ref, f32[2,2176,128]{2,1,0:T(8,128)S(1)} %get-tuple-element.45.refs_0_.refs_1_), custom_call_target="tpu_custom_call" | custom-call | flops 16384000 | bytes 16384000 | tf_op jit(solution)/shard_map/own_planes_next/pallas_call | solution.py:586
  57.4 3.1 %ghost_planes_next.1 = (f32[2,1344,128]{2,1,0:T(8,128)S(1)}, f32[2,2176,128]{2,1,0:T(8,128)S(1)}) custom-call(f32[16,2,32,128]{3,2,1,0:T(8,128)S(1)} %get-tuple-element.39.own_ref, f32[9,2,32,128]{3,2,1,0:T(8,128)S(1)} %collective-permute-done.4.zo_ref, f32[9,2,32,128]{3,2,1,0:T(8,128)S(1)} %collective-permute-done.5.ze_ref, ...), custom_call_target="tpu_custom_call", output_to_operand_aliasing={{0}: (4, {})} | custom-call | flops 32768000 | bytes 32768000 | tf_op jit(solution)/shard_map/ghost_planes_next/pallas_call | solution.py:586
  60.5 1.1 %collective-permute-done.6.yo_ref = f32[2,216,128]{2,1,0:T(8,128)S(1)} collective-permute-done((f32[2,216,128]{2,1,0:T(8,128)S(1)}, f32[2,216,128]{2,1,0:T(8,128)S(1)}, u32[]{:S(2)}, u32[]{:S(2)}) %collective-permute-start.6) | collective-permute-done | bytes 221216 | tf_op jit(solution)/shard_map/ppermute | solution.py:620
  61.6 17.3 %next_step.1 = (f32[16,32,256]{2,1,0:T(8,128)}, f32[2,1344,128]{2,1,0:T(8,128)S(1)}, f32[2,2176,128]{2,1,0:T(8,128)S(1)}) custom-call(f32[2,216,128]{2,1,0:T(8,128)S(1)} %collective-permute-done.6.yo_ref, f32[2,216,128]{2,1,0:T(8,128)S(1)} %collective-permute-done.7.ye_ref, ...), custom_call_target="tpu_custom_call", output_to_operand_aliasing={{1}: (4, {}), {2}: (5, {})} | custom-call | flops 122880000 | bytes 122880000 | tf_op jit(solution)/shard_map/next_step/pallas_call | solution.py:586
  (3 shorter events, 0.0 us)
Async XLA Ops:
  0.0 1.0 %copy-start = (f32[16,32,256]{2,1,0:T(8,128)S(1)}, f32[16,32,256]{2,1,0:T(8,128)}, u32[]{:S(2)}) copy-start(f32[16,32,256]{2,1,0:T(8,128)} %own_ref.1) | copy-start | bytes 1572868
  1.8 11.4 %collective-permute-start = (f32[9,2,32,128]{3,2,1,0:T(8,128)S(1)}, f32[9,2,32,128]{3,2,1,0:T(8,128)S(1)}, u32[]{:S(2)}, u32[]{:S(2)}) collective-permute-start(f32[9,2,32,128]{3,2,1,0:T(8,128)S(1)} %get-tuple-element.28), channel_id=1, source_target_pairs={{8,16},{16,8},{24,32},{32,24},{40,48},{48,40},{56,64},{64,56},{72,... | collective-permute-start | bytes 884744 | tf_op jit(solution)/shard_map/ppermute | solution.py:610
  8.7 4.4 %collective-permute-start.1 = (f32[9,2,32,128]{3,2,1,0:T(8,128)S(1)}, f32[9,2,32,128]{3,2,1,0:T(8,128)S(1)}, u32[]{:S(2)}, u32[]{:S(2)}) collective-permute-start(f32[9,2,32,128]{3,2,1,0:T(8,128)S(1)} %get-tuple-element.29), channel_id=1, source_target_pairs={{0,8},{8,0},{16,24},{24,16},{32,40},{40,32},{48,56},{56,48},{64,72... | collective-permute-start | bytes 884744 | tf_op jit(solution)/shard_map/ppermute | solution.py:611
  13.3 11.1 %collective-permute-start.2 = (f32[2,216,128]{2,1,0:T(8,128)S(1)}, f32[2,216,128]{2,1,0:T(8,128)S(1)}, u32[]{:S(2)}, u32[]{:S(2)}) collective-permute-start(f32[2,216,128]{2,1,0:T(8,128)S(1)} %get-tuple-element.30), channel_id=1, source_target_pairs={{1,2},{2,1},{3,4},{4,3},{5,6},{6,5},{9,10},{10,9},{11,12},{12,11},... | collective-permute-start | bytes 663560 | tf_op jit(solution)/shard_map/ppermute | solution.py:620
  19.1 6.0 %collective-permute-start.3 = (f32[2,216,128]{2,1,0:T(8,128)S(1)}, f32[2,216,128]{2,1,0:T(8,128)S(1)}, u32[]{:S(2)}, u32[]{:S(2)}) collective-permute-start(f32[2,216,128]{2,1,0:T(8,128)S(1)} %get-tuple-element.31), channel_id=1, source_target_pairs={{0,1},{1,0},{2,3},{3,2},{4,5},{5,4},{6,7},{7,6},{8,9},{9,8},{10,11... | collective-permute-start | bytes 663560 | tf_op jit(solution)/shard_map/ppermute | solution.py:621
  41.7 9.8 %collective-permute-start.4 = (f32[9,2,32,128]{3,2,1,0:T(8,128)S(1)}, f32[9,2,32,128]{3,2,1,0:T(8,128)S(1)}, u32[]{:S(2)}, u32[]{:S(2)}) collective-permute-start(f32[9,2,32,128]{3,2,1,0:T(8,128)S(1)} %get-tuple-element.40), channel_id=1, source_target_pairs={{8,16},{16,8},{24,32},{32,24},{40,48},{48,40},{56,64},{64,56},{72,... | collective-permute-start | bytes 884744 | tf_op jit(solution)/shard_map/ppermute | solution.py:610
  45.5 6.0 %collective-permute-start.5 = (f32[9,2,32,128]{3,2,1,0:T(8,128)S(1)}, f32[9,2,32,128]{3,2,1,0:T(8,128)S(1)}, u32[]{:S(2)}, u32[]{:S(2)}) collective-permute-start(f32[9,2,32,128]{3,2,1,0:T(8,128)S(1)} %get-tuple-element.41), channel_id=1, source_target_pairs={{0,8},{8,0},{16,24},{24,16},{32,40},{40,32},{48,56},{56,48},{64,72... | collective-permute-start | bytes 884744 | tf_op jit(solution)/shard_map/ppermute | solution.py:611
  51.7 9.9 %collective-permute-start.6 = (f32[2,216,128]{2,1,0:T(8,128)S(1)}, f32[2,216,128]{2,1,0:T(8,128)S(1)}, u32[]{:S(2)}, u32[]{:S(2)}) collective-permute-start(f32[2,216,128]{2,1,0:T(8,128)S(1)} %get-tuple-element.42), channel_id=1, source_target_pairs={{1,2},{2,1},{3,4},{4,3},{5,6},{6,5},{9,10},{10,9},{11,12},{12,11},... | collective-permute-start | bytes 663560 | tf_op jit(solution)/shard_map/ppermute | solution.py:620
  55.6 6.0 %collective-permute-start.7 = (f32[2,216,128]{2,1,0:T(8,128)S(1)}, f32[2,216,128]{2,1,0:T(8,128)S(1)}, u32[]{:S(2)}, u32[]{:S(2)}) collective-permute-start(f32[2,216,128]{2,1,0:T(8,128)S(1)} %get-tuple-element.43), channel_id=1, source_target_pairs={{0,1},{1,0},{2,3},{3,2},{4,5},{5,4},{6,7},{7,6},{8,9},{9,8},{10,11... | collective-permute-start | bytes 663560 | tf_op jit(solution)/shard_map/ppermute | solution.py:621
